TPU v7x, 32 devices: a whole 2x2x4 slice. The times are simulated.
32 devices in a mesh: gx: 8 (over z, y), gy: 4 (over x, core).
Axes of the slice: x: 2, y: 2, z: 4, core: 2. Of those that a mesh axis runs over, the one named last changes fastest.
Arguments:
- water_depth: float32 [1024, 2048], P('gx', 'gy'), may hold values from 0.5 to 2
- momentum_x: float32 [1024, 2048], P('gx', 'gy'), may hold values from -1.5 to 1.5
- momentum_y: float32 [1024, 2048], P('gx', 'gy'), may hold values from -1.5 to 1.5
- wet_mask: int32 [1024, 2048], P('gx', 'gy'), may hold values from 0 to 1, as said below
- damage_class: int32 [1024, 2048], P('gx', 'gy'), may hold values from 0 to 7
- damage_rates: float32 [8], replicated, may hold values from 0.2 to 2
- dam_cell: int32 [64], replicated, may hold values from 0 to 2097151, as said below
- releases: float32 [64, 2], replicated, may hold values from 0.5 to 4
Outputs:
- final_depth: float32 [1024, 2048], P('gx', 'gy')
- depth_adjoint: float32 [1024, 2048], P('gx', 'gy')
- release_grad: float32 [64, 2], replicated
Inputs may be any that keep to these rules, and one draw needn't show every extreme that they name: Every dam's inflow cell has wet_mask 1. `dam_cell`: a cell index row * 2048 + column.
All inputs are finite; a program needn't handle non-finite values.
Results may differ from a plain program's by a relative error of at most 0.0003.
Values sent between devices are 32-bit elements; how exact they have to be, the bound alone decides.
A program may use at most 64 MiB of HBM per device.

v0:
```python
import functools

import jax
import jax.numpy as jnp
from jax import lax
from jax.experimental import pallas as pl
from jax.experimental.pallas import tpu as pltpu
from jax.sharding import PartitionSpec as P

GRAVITY = 9.81
TIME_RATIO = 0.05
INFLOW_GAIN = 0.25
HALO = 4
LANES = 128
TOP = 8
OWN = TOP + HALO
G_STATIC, G_FIRST, G_LAST, G_BACK_LAST, G_BACK_FIRST = 2, 1, 2, 1, 1
MESH = pl.DeviceIdType.MESH


def speeds(u_l, c_l, u_r, c_r):
    low_l, low_r = u_l - c_l, u_r - c_r
    high_l, high_r = u_l + c_l, u_r + c_r
    return low_l, low_r, high_l, high_r, jnp.minimum(low_l, low_r), jnp.maximum(high_l, high_r)


def sweep(body, first, last, group):
    whole = (last - first) // group

    def run(i, carry):
        base = pl.multiple_of(i * (8 * group), 8)
        for j in range(group):
            body(base + 8 * (first + j))
        return carry

    lax.fori_loop(0, whole, run, 0)
    for chunk in range(first + whole * group, last):
        body(8 * chunk)


def picked_by(values, hot, dims):
    out = None
    for _ in range(3):
        part = values.astype(jnp.bfloat16)
        values = values - part.astype(jnp.float32)
        term = lax.dot_general(part, hot, (dims, ((), ())), preferred_element_type=jnp.float32)
        out = term if out is None else out + term
    return out


def halved_on_tie(value, picks, ties):
    return jnp.where(picks, value, jnp.where(ties, 0.5 * value, 0.0))


def speed_grads(u_l, c_l, u_r, c_r, inverse, slope_of):
    low_l, low_r, high_l, high_r, low, high = speeds(u_l, c_l, u_r, c_r)
    slow, fast = jnp.minimum(low, 0.0), jnp.maximum(high, 0.0)
    alpha = fast * inverse
    beta = -slow * inverse
    gamma = slow * alpha
    d_term, k_term = slope_of
    g_fast = -(inverse * beta) * (d_term - slow * k_term)
    g_slow = -(inverse * alpha) * (d_term - fast * k_term)
    g_slow = halved_on_tie(g_slow, low < 0.0, low == 0.0)
    g_fast = halved_on_tie(g_fast, high > 0.0, high == 0.0)
    slow_l = halved_on_tie(g_slow, low_l < low_r, low_l == low_r)
    slow_r = g_slow - slow_l
    fast_l = halved_on_tie(g_fast, high_l > high_r, high_l == high_r)
    fast_r = g_fast - fast_l
    return (
        alpha,
        beta,
        gamma,
        (fast_l + slow_l, fast_l - slow_l),
        (fast_r + slow_r, fast_r - slow_r),
    )


def kernel(
    n_gx,
    n_gy,
    total_cols,
    classes,
    depth_in,
    mx_in,
    my_in,
    wet_in,
    class_in,
    rates,
    dams,
    releases,
    depth_out,
    adjoint_out,
    grad_out,
    raw_d,
    raw_x,
    raw_y,
    raw_wet,
    raw_cls,
    fields,
    prims,
    statics,
    inverses,
    inflow,
    adj,
    shifted,
    col_hot,
    pack_cols,
    send_rows,
    recv_rows,
    send_cols,
    recv_cols,
    recv_corner,
    gpart,
    gsum,
    recv_gy,
    recv_gx,
    in_sem,
    edge_send,
    edge_recv,
    gy_send,
    gy_recv,
    gx_send,
    gx_recv,
):
    rows, cols = depth_in.shape
    tiles = cols // LANES
    wide = tiles + 1
    span = rows + 2 * HALO
    chunks = span // 8
    ix, iy = lax.axis_index("gx"), lax.axis_index("gy")
    lane = lax.broadcasted_iota(jnp.int32, (8, LANES), 1)

    has_up, has_down = ix > 0, ix < n_gx - 1
    has_left, has_right = iy > 0, iy < n_gy - 1

    loads = []
    for index, (source, target) in enumerate(
        ((depth_in, raw_d), (mx_in, raw_x), (my_in, raw_y), (wet_in, raw_wet), (class_in, raw_cls))
    ):
        for c in range(tiles):
            copy = pltpu.make_async_copy(
                source.at[:, pl.ds(c * LANES, LANES)], target.at[c], in_sem.at[index, c]
            )
            copy.start()
            loads.append(copy)

    barrier = pltpu.get_barrier_semaphore()
    for step in range(1, n_gy):
        pl.semaphore_signal(
            barrier, inc=1, device_id=(ix, lax.rem(iy + step, n_gy)), device_id_type=MESH
        )
    for step in range(1, n_gx):
        pl.semaphore_signal(
            barrier, inc=1, device_id=(lax.rem(ix + step, n_gx), iy), device_id_type=MESH
        )
    sides = (
        (has_up, -1, 0),
        (has_down, 1, 0),
        (has_left, 0, -1),
        (has_right, 0, 1),
        (has_up & has_left, -1, -1),
        (has_up & has_right, -1, 1),
        (has_down & has_left, 1, -1),
        (has_down & has_right, 1, 1),
    )
    corners = 0
    for exists, dx, dy in sides[4:]:
        corners = corners + exists.astype(jnp.int32)

        @pl.when(exists)
        def _(dx=dx, dy=dy):
            pl.semaphore_signal(barrier, inc=1, device_id=(ix + dx, iy + dy), device_id_type=MESH)

    for copy in loads:
        copy.wait()

    rate = [rates[k] for k in range(classes)]

    def coded_chunk(c, start, size=8):
        at = (c, pl.ds(start, size), slice(None))
        wet = raw_wet[at] > 0
        cls = raw_cls[at]
        weight = jnp.full(cls.shape, rate[0])
        for k in range(1, classes):
            weight = jnp.where(cls == k, rate[k], weight)
        return (
            jnp.where(wet, raw_d[at], -1.0),
            raw_x[at],
            raw_y[at],
            jnp.where(wet, weight, 0.0),
        )

    for c in range(tiles):
        for side, start, pick in ((0, 0, 0), (1, rows - 8, 4)):
            four = coded_chunk(c, start)
            for k in range(4):
                send_rows[side, c, 4 * k : 4 * k + 4, :] = four[k][pick : pick + 4]

    def pack_body(i, carry):
        start = pl.multiple_of(i * 8, 8)
        left = coded_chunk(0, start)
        right = coded_chunk(tiles - 1, start)
        packed = jnp.zeros((8, LANES), jnp.float32)
        for k in range(4):
            mine = (lane >= 4 * k) & (lane < 4 * k + 4)
            packed = jnp.where(mine, pltpu.roll(left[k], 4 * k, 1) if k else left[k], packed)
            mine = (lane >= 16 + 4 * k) & (lane < 20 + 4 * k)
            packed = jnp.where(mine, pltpu.roll(right[k], 20 + 4 * k, 1), packed)
        pack_cols[pl.ds(start, 8), :] = packed
        return carry

    lax.fori_loop(0, rows // 8, pack_body, 0, unroll=2)
    turned = jnp.transpose(pack_cols[...])
    send_cols[0] = turned[0:16]
    send_cols[1] = turned[16:32]

    pl.semaphore_wait(barrier, (n_gy - 1) + (n_gx - 1) + corners)

    def edge_copy(index):
        _, dx, dy = sides[index]
        opposite = (1, 0, 3, 2, 7, 6, 5, 4)[index]
        if index < 2:
            source, target = send_rows.at[index], recv_rows.at[opposite]
        elif index < 4:
            source, target = send_cols.at[index - 2], recv_cols.at[opposite - 2]
        else:
            first = 0 if index < 6 else rows - 8
            source, target = pack_cols.at[pl.ds(first, 8), :], recv_corner.at[opposite - 4]
        return pltpu.make_async_remote_copy(
            src_ref=source,
            dst_ref=target,
            send_sem=edge_send.at[index],
            recv_sem=edge_recv.at[opposite],
            device_id=(ix + dx, iy + dy),
            device_id_type=MESH,
        )

    for index in (4, 5, 6, 7, 0, 1, 2, 3):

        @pl.when(sides[index][0])
        def _(index=index):
            edge_copy(index).start()

    H, MX, MY = 0, 1, 2
    UX, UY, CC, QX, QY, TT, IH = range(7)
    WET, WGT, FMX, FMY, WDX, WSX, WDY, WSY = range(8)

    def put_start(c, at_rows, size, four):
        wet = four[0] > 0.0
        at = (c, pl.ds(at_rows, size), slice(None))
        fields[(0, H) + at] = jnp.where(wet, four[0], 1.0)
        fields[(0, MX) + at] = jnp.where(wet, four[1], 0.0)
        fields[(0, MY) + at] = jnp.where(wet, four[2], 0.0)
        statics[(WGT,) + at] = jnp.where(wet, four[3], 0.0)
        statics[(WET,) + at] = jnp.where(wet, 1.0, 0.0)

    def own_body(i, carry):
        start = pl.multiple_of(i * 8, 8)
        for c in range(tiles):
            put_start(c, start + OWN, 8, coded_chunk(c, start))
        return carry

    lax.fori_loop(0, rows // 8, own_body, 0)

    cell = dams[...]
    if total_cols & (total_cols - 1) == 0:
        dam_row = lax.shift_right_logical(cell, total_cols.bit_length() - 1)
    else:
        dam_row = lax.div(cell, total_cols)
    dam_col = cell - dam_row * total_cols
    dam_count = cell.shape[1]
    local_row = dam_row - ix * rows
    local_col = dam_col - iy * cols
    amounts = INFLOW_GAIN * releases[...]
    wide_row = lax.broadcasted_iota(jnp.int32, (span, dam_count), 0) - HALO
    row_hot = wide_row == local_row
    gain_rows = jnp.concatenate(
        [jnp.where(row_hot, amounts[s : s + 1], 0.0) for s in range(2)], axis=0
    )
    position = lax.broadcasted_iota(jnp.int32, (LANES, dam_count), 0)
    for c in range(wide):
        if c < tiles:
            column = position + c * LANES
        else:
            column = jnp.where(
                position < HALO,
                position + cols,
                jnp.where(position >= LANES - HALO, position - LANES, -2 * LANES),
            )
        hot = (column == local_col).astype(jnp.float32).astype(jnp.bfloat16)
        col_hot[c] = hot
        poured = picked_by(gain_rows, hot, ((1,), (1,)))
        inflow[0, c, TOP : TOP + span, :] = poured[:span]
        inflow[1, c, TOP : TOP + span, :] = poured[span:]

    for index in range(8):

        @pl.when(sides[index][0])
        def _(index=index):
            copy = edge_copy(index)
            copy.wait_send()
            opposite = (1, 0, 3, 2, 7, 6, 5, 4)[index]
            if index < 2:
                target = recv_rows.at[index]
            elif index < 4:
                target = recv_cols.at[index - 2]
            else:
                target = recv_corner.at[index - 4]
            pltpu.make_async_copy(target, target, edge_recv.at[index]).wait()

    for c in range(tiles):
        for side, exists, at_rows in ((0, has_up, TOP), (1, has_down, OWN + rows)):
            four = [recv_rows[side, c, 4 * k : 4 * k + 4, :] for k in range(4)]
            four[0] = jnp.where(exists, four[0], -1.0)
            put_start(c, at_rows, 4, four)

    halves = jnp.concatenate(
        [recv_cols[0], recv_cols[1], jnp.zeros((LANES - 32, rows), jnp.float32)], axis=0
    )
    pack_cols[...] = jnp.transpose(halves)

    def rim_tile(left_part, right_part, k, left_at, right_at, from_left, from_right):
        fill = -1.0 if k == 0 else 0.0
        on_right = (lane < HALO) & from_right
        on_left = (lane >= LANES - HALO) & from_left
        shift_r = (LANES - right_at - 4 * k) % LANES
        shift_l = (LANES - HALO - left_at - 4 * k) % LANES
        right_val = pltpu.roll(right_part, shift_r, 1) if shift_r else right_part
        left_val = pltpu.roll(left_part, shift_l, 1) if shift_l else left_part
        return jnp.where(on_right, right_val, jnp.where(on_left, left_val, fill))

    def rim_body(i, carry):
        start = pl.multiple_of(i * 8, 8)
        part = pack_cols[pl.ds(start, 8), :]
        four = [rim_tile(part, part, k, 0, 16, has_left, has_right) for k in range(4)]
        put_start(tiles, start + OWN, 8, four)
        return carry

    lax.fori_loop(0, rows // 8, rim_body, 0, unroll=2)
    for left_slot, right_slot, exists, at_rows, pick in (
        (0, 1, has_up, TOP, 4),
        (2, 3, has_down, OWN + rows, 0),
    ):
        four = [
            rim_tile(
                recv_corner[left_slot],
                recv_corner[right_slot],
                k,
                16,
                0,
                has_left & exists,
                has_right & exists,
            )[pick : pick + 4]
            for k in range(4)
        ]
        put_start(tiles, at_rows, 4, four)

    def next_lanes(values):
        turned_all = [pltpu.roll(value, LANES - 1, 1) for value in values]
        return [
            jnp.where(lane == LANES - 1, turned_all[(c + 1) % wide], turned_all[c])
            for c in range(wide)
        ]

    def with_next(get, k):
        values = [get(k, c) for c in range(wide)]
        return list(zip(values, next_lanes(values)))

    def derived(h, n):
        ih = 1.0 / h
        squared = GRAVITY * h
        return n * ih, squared * lax.rsqrt(squared), ih

    def from_previous(current, previous):
        return jnp.where(
            lane == 0, pltpu.roll(previous, 1, 1), pltpu.roll(current, 1, 1)
        )

    def put_prims(step, c, at, h, mx, my):
        ih = 1.0 / h
        ux, uy = mx * ih, my * ih
        squared = GRAVITY * h
        pressure = 0.5 * squared * h
        values = (
            ux,
            uy,
            squared * lax.rsqrt(squared),
            mx * ux + pressure,
            my * uy + pressure,
            mx * uy,
            ih,
        )
        for k, value in enumerate(values):
            prims[(step, k) + at] = value

    def static_body(row):
        start = row + TOP
        wets = [statics[WET, c, pl.ds(start, 8), :] for c in range(wide)]
        rights = next_lanes(wets)
        for c in range(wide):
            at = (c, pl.ds(start, 8), slice(None))
            wet = wets[c]
            above = statics[WET, c, pl.ds(start - 1, 8), :]
            below = statics[WET, c, pl.ds(start + 1, 8), :]
            right = rights[c]
            left = from_previous(wet, wets[(c - 1) % wide])
            statics[(FMX,) + at] = wet * below
            statics[(FMY,) + at] = wet * right
            statics[(WDX,) + at] = above - below
            statics[(WSX,) + at] = 2.0 - above - below
            statics[(WDY,) + at] = left - right
            statics[(WSY,) + at] = 2.0 - left - right
            put_prims(0, c, at, fields[(0, H) + at], fields[(0, MX) + at], fields[(0, MY) + at])

    sweep(static_body, 0, chunks, G_STATIC)

    def face(u_l, c_l, u_r, c_r, mask):
        low, high = speeds(u_l, c_l, u_r, c_r)[4:]
        slow, fast = jnp.minimum(low, 0.0), jnp.maximum(high, 0.0)
        inverse = mask / (fast - slow)
        alpha = fast * inverse
        return inverse, alpha, slow * inverse, slow * alpha

    def forward_body(step, row):
        start = row + TOP
        last = step == 1
        here = pl.ds(start, 8)
        after = pl.ds(start + 1, 8)
        before = pl.ds(start - 1, 8)

        def f_at(k, c, rows_at=here):
            return fields[step, k, c, rows_at, :]

        def p_at(k, c, rows_at=here):
            return prims[step, k, c, rows_at, :]

        col_h, col_n = with_next(f_at, H), with_next(f_at, MY)
        col_t = None if last else with_next(f_at, MX)

        def col_fluxes(c):
            (h_l, h_r), (n_l, n_r) = col_h[c], col_n[c]
            u_r, c_r, _ = derived(h_r, n_r)
            inverse, alpha, minus_beta, gamma = face(
                p_at(UY, c), p_at(CC, c), u_r, c_r, statics[FMY, c, here, :]
            )
            inverses[step, 1, c, here, :] = inverse
            out = [alpha * n_l - minus_beta * n_r + gamma * (h_r - h_l)]
            if not last:
                t_l, t_r = col_t[c]
                q_r = n_r * u_r + (0.5 * GRAVITY) * h_r * h_r
                out.append(alpha * p_at(QY, c) - minus_beta * q_r + gamma * (n_r - n_l))
                out.append(
                    alpha * p_at(TT, c) - minus_beta * (t_r * u_r) + gamma * (t_r - t_l)
                )
            return out

        previous = col_fluxes(wide - 1)
        for c in range(wide):
            at = (c, here, slice(None))
            h, mx, ux, cc = f_at(H, c), f_at(MX, c), p_at(UX, c), p_at(CC, c)
            h_r, n_r = f_at(H, c, after), f_at(MX, c, after)
            inverse, alpha, minus_beta, gamma = face(
                ux, cc, p_at(UX, c, after), p_at(CC, c, after), statics[FMX, c, here, :]
            )
            inverses[step, 0, c, here, :] = inverse
            row_flux = [alpha * mx - minus_beta * n_r + gamma * (h_r - h)]
            if not last:
                my, qx, tt = f_at(MY, c), p_at(QX, c), p_at(TT, c)
                row_flux.append(
                    alpha * qx - minus_beta * p_at(QX, c, after) + gamma * (n_r - mx)
                )
                row_flux.append(
                    alpha * tt
                    - minus_beta * p_at(TT, c, after)
                    + gamma * (f_at(MY, c, after) - my)
                )
            for k, value in enumerate(row_flux):
                shifted[k, c, here, :] = value
            current = col_fluxes(c) if c < wide - 1 else kept_col
            if c == 0:
                kept_col = previous
            changes = [
                value - shifted[k, c, before, :] + mine - from_previous(mine, other)
                if k == 0
                else None
                for k, (value, mine, other) in enumerate(zip(row_flux, current, previous))
            ]
            wet = statics[WET, c, here, :]
            gain = TIME_RATIO * wet
            new_h = h - gain * changes[0] + inflow[step, c, here, :]
            if last:
                fields[2, H, c, here, :] = new_h
                terminal = statics[WGT, c, here, :] * new_h
                adj[3, c, here, :] = terminal
                adj[4, c, here, :] = gain * terminal
            else:
                uy, qy = p_at(UY, c), p_at(QY, c)
                change_x = (
                    row_flux[1]
                    - shifted[1, c, before, :]
                    + current[2]
                    - from_previous(current[2], previous[2])
                    + statics[WDX, c, here, :] * qx
                    + statics[WSX, c, here, :] * (jnp.abs(ux) + cc) * mx
                )
                change_y = (
                    row_flux[2]
                    - shifted[2, c, before, :]
                    + current[1]
                    - from_previous(current[1], previous[1])
                    + statics[WDY, c, here, :] * qy
                    + statics[WSY, c, here, :] * (jnp.abs(uy) + cc) * my
                )
                new_x = mx - gain * change_x
                new_y = my - gain * change_y
                fields[(1, H) + at] = new_h
                fields[(1, MX) + at] = new_x
                fields[(1, MY) + at] = new_y
                put_prims(1, c, at, new_h, new_x, new_y)
            previous = current

    sweep(functools.partial(forward_body, 0), 0, chunks, G_FIRST)
    sweep(functools.partial(forward_body, 1), 0, chunks, G_LAST)

    def depth_body(i, carry):
        start = pl.multiple_of(i * 8, 8)
        for c in range(tiles):
            own = pl.ds(start + OWN, 8)
            depth_out[pl.ds(start, 8), c * LANES : (c + 1) * LANES] = jnp.where(
                statics[WET, c, own, :] > 0.0, fields[2, H, c, own, :], raw_d[c, pl.ds(start, 8), :]
            )
        return carry

    lax.fori_loop(0, rows // 8, depth_body, 0)
    def backward_last(row):
        start = row + TOP
        here, after, before = pl.ds(start, 8), pl.ds(start + 1, 8), pl.ds(start - 1, 8)

        def f_at(k, c, rows_at=here):
            return fields[1, k, c, rows_at, :]

        def p_at(k, c, rows_at=here):
            return prims[1, k, c, rows_at, :]

        def z_at(k, c, rows_at=here):
            return adj[4, c, rows_at, :]

        def one_face(h, n, u, cc, ih, z, inverse):
            gh = z[1] - z[0]
            slopes = (gh * (n[1] - n[0]), gh * (h[1] - h[0]))
            alpha, beta, gamma, left, right = speed_grads(u[0], cc[0], u[1], cc[1], inverse, slopes)
            jump = gamma * gh
            left_u, right_u = left[0] * ih[0], right[0] * ih[1]
            return (
                0.5 * cc[0] * ih[0] * left[1] - left_u * u[0] - jump,
                alpha * gh + left_u,
            ), (
                0.5 * cc[1] * ih[1] * right[1] - right_u * u[1] + jump,
                beta * gh + right_u,
            )

        col_h, col_n, col_z = with_next(f_at, H), with_next(f_at, MY), with_next(z_at, 0)

        def col_face(c):
            u_r, c_r, ih_r = derived(col_h[c][1], col_n[c][1])
            return one_face(
                col_h[c], col_n[c], (p_at(UY, c), u_r), (p_at(CC, c), c_r), (p_at(IH, c), ih_r),
                col_z[c], inverses[1, 1, c, here, :],
            )

        edge = col_face(wide - 1)
        previous = edge
        for c in range(wide):

            def pair(get, k):
                return get(k, c), get(k, c, after)

            left, right = one_face(
                pair(f_at, H), pair(f_at, MX), pair(p_at, UX), pair(p_at, CC), pair(p_at, IH),
                pair(z_at, 0), inverses[1, 0, c, here, :],
            )
            for k in range(2):
                shifted[k, c, here, :] = right[k]
            in_x = [left[k] + shifted[k, c, before, :] for k in range(2)]
            current = col_face(c) if c < wide - 1 else edge
            in_y = [
                current[0][k] + from_previous(current[1][k], previous[1][k]) for k in range(2)
            ]
            previous = current
            adj_h = adj[3, c, here, :] + in_x[0] + in_y[0]
            gain = TIME_RATIO * statics[WET, c, here, :]
            adj[5, c, here, :] = adj_h
            adj[0, c, here, :] = gain * adj_h
            adj[1, c, here, :] = gain * in_x[1]
            adj[2, c, here, :] = gain * in_y[1]

    sweep(backward_last, 0, chunks, G_BACK_LAST)

    own_hot = lax.broadcasted_iota(jnp.int32, (rows, dam_count), 0) == local_row
    gpart[...] = jnp.zeros(gpart.shape, jnp.float32)
    for s, plane in ((0, 5), (1, 3)):
        picked = jnp.zeros((rows, dam_count), jnp.float32)
        for c in range(tiles):
            picked = picked + picked_by(
                adj[plane, c, OWN : OWN + rows, :], col_hot[c], ((1,), (0,))
            )
        gpart[s : s + 1, 0:dam_count] = INFLOW_GAIN * jnp.sum(
            jnp.where(own_hot, picked, 0.0), axis=0, keepdims=True
        )

    def gy_copy(step):
        return pltpu.make_async_remote_copy(
            src_ref=gpart,
            dst_ref=recv_gy.at[step - 1],
            send_sem=gy_send.at[step - 1],
            recv_sem=gy_recv.at[step - 1],
            device_id=(ix, lax.rem(iy + step, n_gy)),
            device_id_type=MESH,
        )

    def gx_copy(step):
        return pltpu.make_async_remote_copy(
            src_ref=gsum,
            dst_ref=recv_gx.at[step - 1],
            send_sem=gx_send.at[step - 1],
            recv_sem=gx_recv.at[step - 1],
            device_id=(lax.rem(ix + step, n_gx), iy),
            device_id_type=MESH,
        )

    for step in range(1, n_gy):
        gy_copy(step).start()

    def backward_first(row):
        start = row + OWN - 8
        out_row = max(row - 8, 0) if isinstance(row, int) else pl.multiple_of(jnp.maximum(row - 8, 0), 8)
        here, after, before = pl.ds(start, 8), pl.ds(start + 1, 8), pl.ds(start - 1, 8)

        def f_at(k, c, rows_at=here):
            return fields[0, k, c, rows_at, :]

        def p_at(k, c, rows_at=here):
            return prims[0, k, c, rows_at, :]

        def z_at(k, c, rows_at=here):
            return adj[k, c, rows_at, :]

        def one_face(h, n, t, u, cc, ih, q, v, zh, zn, zt, inverse):
            gh, gn, gt = zh[1] - zh[0], zn[1] - zn[0], zt[1] - zt[0]
            dn = n[1] - n[0]
            slopes = (
                gh * dn + gn * (q[1] - q[0]) + gt * (v[1] - v[0]),
                gh * (h[1] - h[0]) + gn * dn + gt * (t[1] - t[0]),
            )
            alpha, beta, gamma, left, right = speed_grads(u[0], cc[0], u[1], cc[1], inverse, slopes)
            jump = gamma * gh
            out = []
            for k, share, (g_u, g_c) in ((0, alpha, left), (1, beta, right)):
                g_u = g_u + share * (gn * n[k] + gt * t[k])
                rest = GRAVITY * h[k] * (share * gn) + ih[k] * (0.5 * cc[k] * g_c - g_u * u[k])
                out.append(rest - jump if k == 0 else rest + jump)
            return out

        col_h, col_n, col_t = with_next(f_at, H), with_next(f_at, MY), with_next(f_at, MX)
        col_zh, col_zn, col_zt = with_next(z_at, 0), with_next(z_at, 2), with_next(z_at, 1)

        def col_face(c):
            h_r, n_r, t_r = col_h[c][1], col_n[c][1], col_t[c][1]
            u_r, c_r, ih_r = derived(h_r, n_r)
            q_r = n_r * u_r + (0.5 * GRAVITY) * h_r * h_r
            return one_face(
                col_h[c], col_n[c], col_t[c], (p_at(UY, c), u_r), (p_at(CC, c), c_r),
                (p_at(IH, c), ih_r), (p_at(QY, c), q_r), (p_at(TT, c), t_r * u_r),
                col_zh[c], col_zn[c], col_zt[c], inverses[0, 1, c, here, :],
            )

        previous = col_face(wide - 1)
        for c in range(tiles):

            def pair(get, k):
                return get(k, c), get(k, c, after)

            left, right = one_face(
                pair(f_at, H), pair(f_at, MX), pair(f_at, MY), pair(p_at, UX), pair(p_at, CC),
                pair(p_at, IH), pair(p_at, QX), pair(p_at, TT), pair(z_at, 0), pair(z_at, 1),
                pair(z_at, 2), inverses[0, 0, c, here, :],
            )
            shifted[0, c, here, :] = right
            current = col_face(c)
            across = left + shifted[0, c, before, :] + current[0]
            across = across + from_previous(current[1], previous[1])
            previous = current
            h, mx, my = f_at(H, c), f_at(MX, c), f_at(MY, c)
            ux, uy, ih = p_at(UX, c), p_at(UY, c), p_at(IH, c)
            zx, zy = z_at(1, c), z_at(2, c)
            normal_x = zx * statics[WDX, c, here, :]
            normal_y = zy * statics[WDY, c, here, :]
            wall_x = zx * statics[WSX, c, here, :] * mx
            wall_y = zy * statics[WSY, c, here, :] * my

            adjoint_out[pl.ds(out_row, 8), c * LANES : (c + 1) * LANES] = (
                adj[5, c, here, :]
                + across
                - GRAVITY * h * (normal_x + normal_y)
                + ih
                * (
                    normal_x * mx * ux
                    + normal_y * my * uy
                    + wall_x * jnp.abs(ux)
                    + wall_y * jnp.abs(uy)
                    - 0.5 * p_at(CC, c) * (wall_x + wall_y)
                )
            )

    runs = rows // 8 + 1
    half = runs // 2 // G_BACK_FIRST * G_BACK_FIRST
    sweep(backward_first, 0, half, G_BACK_FIRST)

    for step in range(1, n_gy):
        gy_copy(step).wait()
    total = gpart[...]
    for step in range(1, n_gy):
        total = total + recv_gy[step - 1]
    gsum[...] = total
    for step in range(1, n_gx):
        gx_copy(step).start()

    sweep(backward_first, half, runs, G_BACK_FIRST)
    for step in range(1, n_gx):
        gx_copy(step).wait()
    for step in range(1, n_gx):
        total = total + recv_gx[step - 1]
    grad_out[...] = total[0:2, 0:dam_count]


def on_device(
    n_gx,
    n_gy,
    water_depth,
    momentum_x,
    momentum_y,
    wet_mask,
    damage_class,
    damage_rates,
    dam_cell,
    releases,
):
    rows, cols = water_depth.shape
    tiles = cols // LANES
    wide = tiles + 1
    high = rows + 2 * HALO + 2 * TOP
    dam_count = dam_cell.shape[0]
    f32 = jnp.float32
    plane = (wide, high, LANES)
    own = (tiles, rows, LANES)
    anywhere = pl.BlockSpec(memory_space=pl.ANY)
    vmem = pl.BlockSpec(memory_space=pltpu.VMEM)
    dma = pltpu.SemaphoreType.DMA
    final_depth, adjoint, grad = pl.pallas_call(
        functools.partial(kernel, n_gx, n_gy, cols * n_gy, damage_rates.shape[0]),
        out_shape=(
            pltpu.VMEM((rows, cols), f32),
            pltpu.VMEM((rows, cols), f32),
            pltpu.VMEM(releases.shape[::-1], f32),
        ),
        in_specs=[anywhere] * 5 + [pl.BlockSpec(memory_space=pltpu.SMEM), vmem, vmem],
        out_specs=(vmem, vmem, vmem),
        scratch_shapes=[
            pltpu.VMEM(own, f32),
            pltpu.VMEM(own, f32),
            pltpu.VMEM(own, f32),
            pltpu.VMEM(own, jnp.int32),
            pltpu.VMEM(own, jnp.int32),
            pltpu.VMEM((3, 3) + plane, f32),
            pltpu.VMEM((2, 7) + plane, f32),
            pltpu.VMEM((8,) + plane, f32),
            pltpu.VMEM((2, 2) + plane, f32),
            pltpu.VMEM((2,) + plane, f32),
            pltpu.VMEM((6,) + plane, f32),
            pltpu.VMEM((3,) + plane, f32),
            pltpu.VMEM((wide, LANES, dam_count), jnp.bfloat16),
            pltpu.VMEM((rows, LANES), f32),
            pltpu.VMEM((2, tiles, 16, LANES), f32),
            pltpu.VMEM((2, tiles, 16, LANES), f32),
            pltpu.VMEM((2, 16, rows), f32),
            pltpu.VMEM((2, 16, rows), f32),
            pltpu.VMEM((4, 8, LANES), f32),
            pltpu.VMEM((8, LANES), f32),
            pltpu.VMEM((8, LANES), f32),
            pltpu.VMEM((n_gy - 1, 8, LANES), f32),
            pltpu.VMEM((n_gx - 1, 8, LANES), f32),
            dma((5, tiles)),
            dma((8,)),
            dma((8,)),
            dma((n_gy - 1,)),
            dma((n_gy - 1,)),
            dma((n_gx - 1,)),
            dma((n_gx - 1,)),
        ],
        compiler_params=pltpu.CompilerParams(
            collective_id=0, has_side_effects=True, vmem_limit_bytes=56 * 1024 * 1024
        ),
        name="window",
    )(
        water_depth,
        momentum_x,
        momentum_y,
        wet_mask,
        damage_class,
        damage_rates,
        dam_cell.reshape(1, dam_count),
        releases.T,
    )
    return final_depth, adjoint, grad.T


def solution(mesh):
    n_gx, n_gy = mesh.shape["gx"], mesh.shape["gy"]
    grid = P("gx", "gy")
    return jax.shard_map(
        functools.partial(on_device, n_gx, n_gy),
        mesh=mesh,
        in_specs=(grid,) * 5 + (P(),) * 3,
        out_specs=(grid, grid, P()),
        check_vma=False,
    )
```

profile of v0, /device:TPU:0, one launch (start us, length us, event | category | flops | bytes accessed | tf_op | source)
XLA Modules:
  0.0 30.4 jit_solution(570752755412169156)
XLA Ops:
  0.6 27.8 %window.1 = (f32[128,512]{1,0:T(8,128)S(1)}, f32[128,512]{1,0:T(8,128)S(1)}, f32[2,64]{1,0:T(2,128)S(1)}) custom-call(f32[128,512]{1,0:T(8,128)} %depth_in.1, f32[128,512]{1,0:T(8,128)} %mx_in.1, f32[128,512]{1,0:T(8,128)} %my_in.1, s32[128,512]{1,0:T(8,128)} %wet_in.1, s32[128,512]{1,0:T(8,128)} %class_in.1, f32[8]{0:T(128)} %rates.1, s32[1,64]{1,0:T(1,128)} %bitcast.5, ...), custom_call_target="tpu_custom_call" | custom-call | tf_op jit(solution)/shard_map/window/pallas_call | solution.py:760
  28.4 0.7 %copy.14 = f32[128,512]{1,0:T(8,128)} copy(f32[128,512]{1,0:T(8,128)S(1)} %get-tuple-element.9) | data formatting | bytes 524288
  29.1 0.6 %copy.16 = f32[64,2]{0,1:T(2,128)} copy(f32[64,2]{0,1:T(2,128)S(1)} %bitcast.3) | data formatting | bytes 1024
  29.7 0.7 %copy.15 = f32[128,512]{1,0:T(8,128)} copy(f32[128,512]{1,0:T(8,128)S(1)} %get-tuple-element.10) | data formatting | bytes 524288
where the time goes:
time: 30.6 us; the launch traced here: 30.4 us
  Pallas kernels  27.8 us (91%)
  local copies, waits for them, and re-layouts  1.97 us (6%)
  between operations  0.64 us (2%)
    pallas_call x1, Pallas kernels, on_device(): pl.pallas_call(functools.partial(kernel, n_gx, n_gy, cols * n_gy, damage_...  27.8 us
    unnamed x3, local copies, waits for them, and re-layouts  1.97 us

commit v1 on v0

--- a/solution.py
+++ b/solution.py
@@ -86,9 +86,9 @@
     my_in,
     wet_in,
     class_in,
-    rates,
-    dams,
-    releases,
+    rates_in,
+    dams_in,
+    releases_in,
     depth_out,
     adjoint_out,
     grad_out,
@@ -115,6 +115,11 @@
     gsum,
     recv_gy,
     recv_gx,
+    rates,
+    dams,
+    releases,
+    small_sem,
+    know_sem,
     in_sem,
     edge_send,
     edge_recv,
@@ -134,25 +139,10 @@
     has_up, has_down = ix > 0, ix < n_gx - 1
     has_left, has_right = iy > 0, iy < n_gy - 1
 
-    loads = []
-    for index, (source, target) in enumerate(
-        ((depth_in, raw_d), (mx_in, raw_x), (my_in, raw_y), (wet_in, raw_wet), (class_in, raw_cls))
-    ):
-        for c in range(tiles):
-            copy = pltpu.make_async_copy(
-                source.at[:, pl.ds(c * LANES, LANES)], target.at[c], in_sem.at[index, c]
-            )
-            copy.start()
-            loads.append(copy)
-
     barrier = pltpu.get_barrier_semaphore()
     for step in range(1, n_gy):
         pl.semaphore_signal(
             barrier, inc=1, device_id=(ix, lax.rem(iy + step, n_gy)), device_id_type=MESH
-        )
-    for step in range(1, n_gx):
-        pl.semaphore_signal(
-            barrier, inc=1, device_id=(lax.rem(ix + step, n_gx), iy), device_id_type=MESH
         )
     sides = (
         (has_up, -1, 0),
@@ -165,15 +155,37 @@
         (has_down & has_right, 1, 1),
     )
     corners = 0
-    for exists, dx, dy in sides[4:]:
+    for exists, dx, dy in sides[:2] + sides[4:]:
         corners = corners + exists.astype(jnp.int32)
 
         @pl.when(exists)
         def _(dx=dx, dy=dy):
             pl.semaphore_signal(barrier, inc=1, device_id=(ix + dx, iy + dy), device_id_type=MESH)
 
+    small = [
+        pltpu.make_async_copy(source, target, small_sem.at[index])
+        for index, (source, target) in enumerate(
+            ((rates_in, rates), (dams_in, dams), (releases_in, releases))
+        )
+    ]
+    for copy in small[:1]:
+        copy.start()
+    loads = []
+    for c in (0, tiles - 1, *range(1, tiles - 1)):
+        for index, (source, target) in enumerate(
+            ((wet_in, raw_wet), (class_in, raw_cls), (depth_in, raw_d), (mx_in, raw_x), (my_in, raw_y))
+        ):
+            copy = pltpu.make_async_copy(
+                source.at[:, pl.ds(c * LANES, LANES)], target.at[c], in_sem.at[index, c]
+            )
+            copy.start()
+            loads.append(copy)
+    for copy in small[1:]:
+        copy.start()
+
     for copy in loads:
         copy.wait()
+    small[0].wait()
 
     rate = [rates[k] for k in range(classes)]
 
@@ -215,7 +227,26 @@
     send_cols[0] = turned[0:16]
     send_cols[1] = turned[16:32]
 
-    pl.semaphore_wait(barrier, (n_gy - 1) + (n_gx - 1) + corners)
+    pl.semaphore_wait(barrier, (n_gy - 1) + corners)
+
+    rounds = max(n_gx - 2, 0).bit_length()
+
+    def reach(level):
+        return (ix >= 2**level, -(2**level)), (ix + 2**level < n_gx, 2**level)
+
+    def tell(level):
+        for exists, offset in reach(level):
+
+            @pl.when(exists)
+            def _(offset=offset):
+                pl.semaphore_signal(
+                    know_sem.at[level], inc=1, device_id=(ix + offset, iy), device_id_type=MESH
+                )
+
+    def learn(level):
+        pl.semaphore_wait(
+            know_sem.at[level], sum(exists.astype(jnp.int32) for exists, _ in reach(level))
+        )
 
     def edge_copy(index):
         _, dx, dy = sides[index]
@@ -242,6 +273,9 @@
         def _(index=index):
             edge_copy(index).start()
 
+    if rounds > 0:
+        tell(0)
+
     H, MX, MY = 0, 1, 2
     UX, UY, CC, QX, QY, TT, IH = range(7)
     WET, WGT, FMX, FMY, WDX, WSX, WDY, WSY = range(8)
@@ -263,6 +297,8 @@
 
     lax.fori_loop(0, rows // 8, own_body, 0)
 
+    for copy in small[1:]:
+        copy.wait()
     cell = dams[...]
     if total_cols & (total_cols - 1) == 0:
         dam_row = lax.shift_right_logical(cell, total_cols.bit_length() - 1)
@@ -308,6 +344,11 @@
             else:
                 target = recv_corner.at[index - 4]
             pltpu.make_async_copy(target, target, edge_recv.at[index]).wait()
+
+    if rounds > 0:
+        learn(0)
+        if rounds > 1:
+            tell(1)
 
     for c in range(tiles):
         for side, exists, at_rows in ((0, has_up, TOP), (1, has_down, OWN + rows)):
@@ -521,6 +562,10 @@
             previous = current
 
     sweep(functools.partial(forward_body, 0), 0, chunks, G_FIRST)
+    if rounds > 1:
+        learn(1)
+        if rounds > 2:
+            tell(2)
     sweep(functools.partial(forward_body, 1), 0, chunks, G_LAST)
 
     def depth_body(i, carry):
@@ -723,6 +768,10 @@
     for step in range(1, n_gy):
         total = total + recv_gy[step - 1]
     gsum[...] = total
+    for level in range(2, rounds):
+        learn(level)
+        if level + 1 < rounds:
+            tell(level + 1)
     for step in range(1, n_gx):
         gx_copy(step).start()
 
@@ -764,7 +813,7 @@
             pltpu.VMEM((rows, cols), f32),
             pltpu.VMEM(releases.shape[::-1], f32),
         ),
-        in_specs=[anywhere] * 5 + [pl.BlockSpec(memory_space=pltpu.SMEM), vmem, vmem],
+        in_specs=[anywhere] * 8,
         out_specs=(vmem, vmem, vmem),
         scratch_shapes=[
             pltpu.VMEM(own, f32),
@@ -790,6 +839,11 @@
             pltpu.VMEM((8, LANES), f32),
             pltpu.VMEM((n_gy - 1, 8, LANES), f32),
             pltpu.VMEM((n_gx - 1, 8, LANES), f32),
+            pltpu.SMEM(damage_rates.shape, f32),
+            pltpu.VMEM((1, dam_count), jnp.int32),
+            pltpu.VMEM(releases.shape[::-1], f32),
+            dma((3,)),
+            pltpu.SemaphoreType.REGULAR((max(n_gx - 2, 1).bit_length(),)),
             dma((5, tiles)),
             dma((8,)),
             dma((8,)),

time: 30.6 us -> 30 us (0.980)
  Pallas kernels: 27.8 us -> 27.2 us
    pallas_call x1, Pallas kernels: 27.8 us -> 27.2 us  [on_device(): pl.pallas_call(functools.partial(kernel, n_gx, n_gy, cols * n_gy, damage_...]
where the time goes in v1:
time: 30 us; the launch traced here: 29.9 us
  Pallas kernels  27.2 us (91%)
  local copies, waits for them, and re-layouts  1.97 us (7%)
  between operations  0.64 us (2%)
    pallas_call x1, Pallas kernels, on_device(): pl.pallas_call(functools.partial(kernel, n_gx, n_gy, cols * n_gy, damage_...  27.2 us
    unnamed x3, local copies, waits for them, and re-layouts  1.97 us

profile of v1, /device:TPU:0, one launch (start us, length us, event | category | flops | bytes accessed | tf_op | source)
XLA Modules:
  0.0 29.9 jit_solution(5041504992451835767)
XLA Ops:
  0.6 27.2 %window.1 = (f32[128,512]{1,0:T(8,128)S(1)}, f32[128,512]{1,0:T(8,128)S(1)}, f32[2,64]{1,0:T(2,128)S(1)}) custom-call(f32[128,512]{1,0:T(8,128)} %depth_in.1, f32[128,512]{1,0:T(8,128)} %mx_in.1, f32[128,512]{1,0:T(8,128)} %my_in.1, s32[128,512]{1,0:T(8,128)} %wet_in.1, s32[128,512]{1,0:T(8,128)} %class_in.1, f32[8]{0:T(128)} %rates_in.1, s32[1,64]{1,0:T(1,128)} %bitcast.5, ...), custom_call_target="tpu_custom_call" | custom-call | tf_op jit(solution)/shard_map/window/pallas_call | solution.py:809
  27.9 0.7 %copy.14 = f32[128,512]{1,0:T(8,128)} copy(f32[128,512]{1,0:T(8,128)S(1)} %get-tuple-element.9) | data formatting | bytes 524288
  28.6 0.6 %copy.16 = f32[64,2]{0,1:T(2,128)} copy(f32[64,2]{0,1:T(2,128)S(1)} %bitcast.3) | data formatting | bytes 1024
  29.2 0.7 %copy.15 = f32[128,512]{1,0:T(8,128)} copy(f32[128,512]{1,0:T(8,128)S(1)} %get-tuple-element.10) | data formatting | bytes 524288

commit v2 on v1

--- a/solution.py
+++ b/solution.py
@@ -18,12 +18,6 @@
 MESH = pl.DeviceIdType.MESH
 
 
-def speeds(u_l, c_l, u_r, c_r):
-    low_l, low_r = u_l - c_l, u_r - c_r
-    high_l, high_r = u_l + c_l, u_r + c_r
-    return low_l, low_r, high_l, high_r, jnp.minimum(low_l, low_r), jnp.maximum(high_l, high_r)
-
-
 def sweep(body, first, last, group):
     whole = (last - first) // group
 
@@ -52,28 +46,13 @@
     return jnp.where(picks, value, jnp.where(ties, 0.5 * value, 0.0))
 
 
-def speed_grads(u_l, c_l, u_r, c_r, inverse, slope_of):
-    low_l, low_r, high_l, high_r, low, high = speeds(u_l, c_l, u_r, c_r)
-    slow, fast = jnp.minimum(low, 0.0), jnp.maximum(high, 0.0)
-    alpha = fast * inverse
-    beta = -slow * inverse
-    gamma = slow * alpha
-    d_term, k_term = slope_of
-    g_fast = -(inverse * beta) * (d_term - slow * k_term)
-    g_slow = -(inverse * alpha) * (d_term - fast * k_term)
-    g_slow = halved_on_tie(g_slow, low < 0.0, low == 0.0)
-    g_fast = halved_on_tie(g_fast, high > 0.0, high == 0.0)
-    slow_l = halved_on_tie(g_slow, low_l < low_r, low_l == low_r)
-    slow_r = g_slow - slow_l
-    fast_l = halved_on_tie(g_fast, high_l > high_r, high_l == high_r)
-    fast_r = g_fast - fast_l
-    return (
-        alpha,
-        beta,
-        gamma,
-        (fast_l + slow_l, fast_l - slow_l),
-        (fast_r + slow_r, fast_r - slow_r),
-    )
+def split_speed_grads(lm_l, lm_r, lp_l, lp_r, coefs, d_term, k_term):
+    _, _, _, slow, fast, e_slow, e_fast = coefs
+    g_slow = e_slow * (fast * k_term - d_term)
+    g_fast = e_fast * (d_term - slow * k_term)
+    slow_l = halved_on_tie(g_slow, lm_l < lm_r, lm_l == lm_r)
+    fast_l = halved_on_tie(g_fast, lp_l > lp_r, lp_l == lp_r)
+    return fast_l, slow_l, g_fast - fast_l, g_slow - slow_l
 
 
 def kernel(
@@ -97,13 +76,15 @@
     raw_y,
     raw_wet,
     raw_cls,
-    fields,
-    prims,
+    first,
+    second,
     statics,
-    inverses,
+    faces,
     inflow,
     adj,
-    shifted,
+    last_h,
+    row_flux,
+    col_flux,
     col_hot,
     pack_cols,
     send_rows,
@@ -276,16 +257,19 @@
     if rounds > 0:
         tell(0)
 
-    H, MX, MY = 0, 1, 2
-    UX, UY, CC, QX, QY, TT, IH = range(7)
-    WET, WGT, FMX, FMY, WDX, WSX, WDY, WSY = range(8)
+    H, MX, MY, LMX, LPX, LMY, LPY, PX, RX, PY, RY = range(11)
+    IH = 11
+    QX, QY, TT, AX, AY, UV, WX, WY, BX, BY = range(11, 21)
+    NEXT = 21
+    WET, WGT, FMX, FMY = range(4)
+    ALPHA, BETA, GAMMA, SLOW, FAST, ESLOW, EFAST = range(7)
 
     def put_start(c, at_rows, size, four):
         wet = four[0] > 0.0
         at = (c, pl.ds(at_rows, size), slice(None))
-        fields[(0, H) + at] = jnp.where(wet, four[0], 1.0)
-        fields[(0, MX) + at] = jnp.where(wet, four[1], 0.0)
-        fields[(0, MY) + at] = jnp.where(wet, four[2], 0.0)
+        first[(H,) + at] = jnp.where(wet, four[0], 1.0)
+        first[(MX,) + at] = jnp.where(wet, four[1], 0.0)
+        first[(MY,) + at] = jnp.where(wet, four[2], 0.0)
         statics[(WGT,) + at] = jnp.where(wet, four[3], 0.0)
         statics[(WET,) + at] = jnp.where(wet, 1.0, 0.0)
 
@@ -404,176 +388,195 @@
             for c in range(wide)
         ]
 
-    def with_next(get, k):
-        values = [get(k, c) for c in range(wide)]
-        return list(zip(values, next_lanes(values)))
-
-    def derived(h, n):
-        ih = 1.0 / h
-        squared = GRAVITY * h
-        return n * ih, squared * lax.rsqrt(squared), ih
-
-    def from_previous(current, previous):
-        return jnp.where(
-            lane == 0, pltpu.roll(previous, 1, 1), pltpu.roll(current, 1, 1)
-        )
-
-    def put_prims(step, c, at, h, mx, my):
-        ih = 1.0 / h
+    def last_lanes(values):
+        turned_all = [pltpu.roll(value, 1, 1) for value in values]
+        return [
+            jnp.where(lane == 0, turned_all[(c - 1) % wide], turned_all[c]) for c in range(wide)
+        ]
+
+    def put_next(target, offset, here, columns):
+        for k, values in columns.items():
+            for c, value in enumerate(next_lanes(values)):
+                target[offset + k, c, here, :] = value
+
+    FIRST_NEXT = (H, MX, MY, LMY, LPY, QY, TT, AY, UV, PY, RY)
+    SECOND_NEXT = (H, MY, LMY, LPY, PY, RY, IH)
+
+    def base_prims(target, c, here, h, mx, my, ih):
         ux, uy = mx * ih, my * ih
         squared = GRAVITY * h
-        pressure = 0.5 * squared * h
-        values = (
-            ux,
-            uy,
-            squared * lax.rsqrt(squared),
-            mx * ux + pressure,
-            my * uy + pressure,
-            mx * uy,
-            ih,
-        )
-        for k, value in enumerate(values):
-            prims[(step, k) + at] = value
+        cc = squared * lax.rsqrt(squared)
+        half = 0.5 * cc
+        out = {H: h, MX: mx, MY: my, LMX: ux - cc, LPX: ux + cc, LMY: uy - cc, LPY: uy + cc}
+        half_i, ux_i, uy_i = half * ih, ux * ih, uy * ih
+        out |= {PX: half_i - ux_i, RX: half_i + ux_i, PY: half_i - uy_i, RY: half_i + uy_i}
+        return out, ux, uy, squared, cc, half
 
     def static_body(row):
         start = row + TOP
-        wets = [statics[WET, c, pl.ds(start, 8), :] for c in range(wide)]
-        rights = next_lanes(wets)
+        here = pl.ds(start, 8)
+        wets = [statics[WET, c, here, :] for c in range(wide)]
+        rights, lefts = next_lanes(wets), last_lanes(wets)
+        kept = {k: [] for k in FIRST_NEXT}
         for c in range(wide):
-            at = (c, pl.ds(start, 8), slice(None))
             wet = wets[c]
             above = statics[WET, c, pl.ds(start - 1, 8), :]
             below = statics[WET, c, pl.ds(start + 1, 8), :]
-            right = rights[c]
-            left = from_previous(wet, wets[(c - 1) % wide])
-            statics[(FMX,) + at] = wet * below
-            statics[(FMY,) + at] = wet * right
-            statics[(WDX,) + at] = above - below
-            statics[(WSX,) + at] = 2.0 - above - below
-            statics[(WDY,) + at] = left - right
-            statics[(WSY,) + at] = 2.0 - left - right
-            put_prims(0, c, at, fields[(0, H) + at], fields[(0, MX) + at], fields[(0, MY) + at])
+            scale = TIME_RATIO * wet
+            statics[FMX, c, here, :] = scale * below
+            statics[FMY, c, here, :] = scale * rights[c]
+            h, mx, my = (first[k, c, here, :] for k in (H, MX, MY))
+            ih = 1.0 / h
+            out, ux, uy, squared, cc, half = base_prims(first, c, here, h, mx, my, ih)
+            pressure = 0.5 * squared * h
+            out[QX], out[QY], out[TT] = mx * ux + pressure, my * uy + pressure, mx * uy
+            out[AX], out[AY], out[UV] = squared - ux * ux, squared - uy * uy, ux * uy
+            for lower, upper, u, n, q, a, wall, back in (
+                (above, below, ux, mx, QX, AX, WX, BX),
+                (lefts[c], rights[c], uy, my, QY, AY, WY, BY),
+            ):
+                single = scale * (lower - upper)
+                both = scale * (2.0 - (lower + upper))
+                size = jnp.abs(u)
+                out[wall] = single * out[q] + both * ((size + cc) * n)
+                out[back] = single * out[a] + both * (u * (half - size))
+            for k, value in out.items():
+                if k not in (H, MX, MY):
+                    first[k, c, here, :] = value
+            for k in FIRST_NEXT:
+                kept[k].append(out[k])
+        put_next(first, 0, here, {NEXT + j: kept[k] for j, k in enumerate(FIRST_NEXT)})
 
     sweep(static_body, 0, chunks, G_STATIC)
 
-    def face(u_l, c_l, u_r, c_r, mask):
-        low, high = speeds(u_l, c_l, u_r, c_r)[4:]
+    def reader(source, keys):
+        def at(k, c, rows_at):
+            return source[k, c, rows_at, :]
+
+        def right(k, c, rows_at):
+            return source[NEXT_OF[id(keys)] + keys.index(k), c, rows_at, :]
+
+        return at, right
+
+    SECOND_AT = 12
+    NEXT_OF = {id(FIRST_NEXT): NEXT, id(SECOND_NEXT): SECOND_AT}
+    f_at, f_right = reader(first, FIRST_NEXT)
+    s_at, s_right = reader(second, SECOND_NEXT)
+
+    def face(step, dim, c, here, lm_l, lm_r, lp_l, lp_r):
+        low, high = jnp.minimum(lm_l, lm_r), jnp.maximum(lp_l, lp_r)
         slow, fast = jnp.minimum(low, 0.0), jnp.maximum(high, 0.0)
-        inverse = mask / (fast - slow)
-        alpha = fast * inverse
-        return inverse, alpha, slow * inverse, slow * alpha
-
-    def forward_body(step, row):
+        inverse = 1.0 / (fast - slow)
+        masked = statics[FMX + dim, c, here, :] * inverse
+        alpha, beta = fast * masked, slow * masked
+        gamma = slow * alpha
+        e_slow = halved_on_tie(alpha * inverse, low < 0.0, low == 0.0)
+        e_fast = halved_on_tie(beta * inverse, high > 0.0, high == 0.0)
+        for k, value in enumerate((alpha, beta, gamma, slow, fast, e_slow, e_fast)):
+            faces[step, dim, k, c, here, :] = value
+        return alpha, beta, gamma
+
+    def coefs_of(step, dim, c, here):
+        return [faces[step, dim, k, c, here, :] for k in range(7)]
+
+    def crossing(coefs, flux_l, flux_r, held_l, held_r):
+        alpha, beta, gamma = coefs
+        return alpha * flux_l - beta * flux_r + gamma * (held_r - held_l)
+
+    def forward_first(row):
         start = row + TOP
-        last = step == 1
-        here = pl.ds(start, 8)
-        after = pl.ds(start + 1, 8)
-        before = pl.ds(start - 1, 8)
-
-        def f_at(k, c, rows_at=here):
-            return fields[step, k, c, rows_at, :]
-
-        def p_at(k, c, rows_at=here):
-            return prims[step, k, c, rows_at, :]
-
-        col_h, col_n = with_next(f_at, H), with_next(f_at, MY)
-        col_t = None if last else with_next(f_at, MX)
-
-        def col_fluxes(c):
-            (h_l, h_r), (n_l, n_r) = col_h[c], col_n[c]
-            u_r, c_r, _ = derived(h_r, n_r)
-            inverse, alpha, minus_beta, gamma = face(
-                p_at(UY, c), p_at(CC, c), u_r, c_r, statics[FMY, c, here, :]
-            )
-            inverses[step, 1, c, here, :] = inverse
-            out = [alpha * n_l - minus_beta * n_r + gamma * (h_r - h_l)]
-            if not last:
-                t_l, t_r = col_t[c]
-                q_r = n_r * u_r + (0.5 * GRAVITY) * h_r * h_r
-                out.append(alpha * p_at(QY, c) - minus_beta * q_r + gamma * (n_r - n_l))
-                out.append(
-                    alpha * p_at(TT, c) - minus_beta * (t_r * u_r) + gamma * (t_r - t_l)
+        here, after, before = pl.ds(start, 8), pl.ds(start + 1, 8), pl.ds(start - 1, 8)
+        cols = []
+        for c in range(wide):
+            coefs = face(
+                0, 1, c, here, f_at(LMY, c, here), f_right(LMY, c, here),
+                f_at(LPY, c, here), f_right(LPY, c, here),
+            )
+            cols.append([
+                crossing(
+                    coefs, f_at(flux, c, here), f_right(flux, c, here),
+                    f_at(held, c, here), f_right(held, c, here),
                 )
-            return out
-
-        previous = col_fluxes(wide - 1)
+                for flux, held in ((MY, H), (TT, MX), (QY, MY))
+            ])
+        entering = [last_lanes([cols[c][k] for c in range(wide)]) for k in range(3)]
+        kept = {k: [] for k in SECOND_NEXT}
         for c in range(wide):
-            at = (c, here, slice(None))
-            h, mx, ux, cc = f_at(H, c), f_at(MX, c), p_at(UX, c), p_at(CC, c)
-            h_r, n_r = f_at(H, c, after), f_at(MX, c, after)
-            inverse, alpha, minus_beta, gamma = face(
-                ux, cc, p_at(UX, c, after), p_at(CC, c, after), statics[FMX, c, here, :]
-            )
-            inverses[step, 0, c, here, :] = inverse
-            row_flux = [alpha * mx - minus_beta * n_r + gamma * (h_r - h)]
-            if not last:
-                my, qx, tt = f_at(MY, c), p_at(QX, c), p_at(TT, c)
-                row_flux.append(
-                    alpha * qx - minus_beta * p_at(QX, c, after) + gamma * (n_r - mx)
+            coefs = face(
+                0, 0, c, here, f_at(LMX, c, here), f_at(LMX, c, after),
+                f_at(LPX, c, here), f_at(LPX, c, after),
+            )
+            new = []
+            for k, (flux, held) in enumerate(((MX, H), (QX, MX), (TT, MY))):
+                value = crossing(
+                    coefs, f_at(flux, c, here), f_at(flux, c, after),
+                    f_at(held, c, here), f_at(held, c, after),
                 )
-                row_flux.append(
-                    alpha * tt
-                    - minus_beta * p_at(TT, c, after)
-                    + gamma * (f_at(MY, c, after) - my)
+                row_flux[k, c, here, :] = value
+                change = value - row_flux[k, c, before, :] + (cols[c][k] - entering[k][c])
+                if k > 0:
+                    change = change + f_at((None, WX, WY)[k], c, here)
+                new.append(f_at((H, MX, MY)[k], c, here) - change)
+            h = new[0] + inflow[0, c, here, :]
+            ih = 1.0 / h
+            out = base_prims(second, c, here, h, new[1], new[2], ih)[0]
+            out[IH] = ih
+            for k, value in out.items():
+                second[k, c, here, :] = value
+            for k in SECOND_NEXT:
+                kept[k].append(out[k])
+        put_next(second, 0, here, {SECOND_AT + j: kept[k] for j, k in enumerate(SECOND_NEXT)})
+
+    TERM, ADJ, ZX, ZY, TERM_R, ADJ_R, ZX_R, ZY_R = range(8)
+
+    def forward_last(row):
+        start = row + TOP
+        here, after, before = pl.ds(start, 8), pl.ds(start + 1, 8), pl.ds(start - 1, 8)
+        cols = []
+        for c in range(wide):
+            coefs = face(
+                1, 1, c, here, s_at(LMY, c, here), s_right(LMY, c, here),
+                s_at(LPY, c, here), s_right(LPY, c, here),
+            )
+            cols.append(
+                crossing(
+                    coefs, s_at(MY, c, here), s_right(MY, c, here),
+                    s_at(H, c, here), s_right(H, c, here),
                 )
-            for k, value in enumerate(row_flux):
-                shifted[k, c, here, :] = value
-            current = col_fluxes(c) if c < wide - 1 else kept_col
-            if c == 0:
-                kept_col = previous
-            changes = [
-                value - shifted[k, c, before, :] + mine - from_previous(mine, other)
-                if k == 0
-                else None
-                for k, (value, mine, other) in enumerate(zip(row_flux, current, previous))
-            ]
-            wet = statics[WET, c, here, :]
-            gain = TIME_RATIO * wet
-            new_h = h - gain * changes[0] + inflow[step, c, here, :]
-            if last:
-                fields[2, H, c, here, :] = new_h
-                terminal = statics[WGT, c, here, :] * new_h
-                adj[3, c, here, :] = terminal
-                adj[4, c, here, :] = gain * terminal
-            else:
-                uy, qy = p_at(UY, c), p_at(QY, c)
-                change_x = (
-                    row_flux[1]
-                    - shifted[1, c, before, :]
-                    + current[2]
-                    - from_previous(current[2], previous[2])
-                    + statics[WDX, c, here, :] * qx
-                    + statics[WSX, c, here, :] * (jnp.abs(ux) + cc) * mx
-                )
-                change_y = (
-                    row_flux[2]
-                    - shifted[2, c, before, :]
-                    + current[1]
-                    - from_previous(current[1], previous[1])
-                    + statics[WDY, c, here, :] * qy
-                    + statics[WSY, c, here, :] * (jnp.abs(uy) + cc) * my
-                )
-                new_x = mx - gain * change_x
-                new_y = my - gain * change_y
-                fields[(1, H) + at] = new_h
-                fields[(1, MX) + at] = new_x
-                fields[(1, MY) + at] = new_y
-                put_prims(1, c, at, new_h, new_x, new_y)
-            previous = current
-
-    sweep(functools.partial(forward_body, 0), 0, chunks, G_FIRST)
+            )
+        entering = last_lanes(cols)
+        terms = []
+        for c in range(wide):
+            coefs = face(
+                1, 0, c, here, s_at(LMX, c, here), s_at(LMX, c, after),
+                s_at(LPX, c, here), s_at(LPX, c, after),
+            )
+            value = crossing(
+                coefs, s_at(MX, c, here), s_at(MX, c, after),
+                s_at(H, c, here), s_at(H, c, after),
+            )
+            row_flux[0, c, here, :] = value
+            change = value - row_flux[0, c, before, :] + (cols[c] - entering[c])
+            h = s_at(H, c, here) - change + inflow[1, c, here, :]
+            last_h[c, here, :] = h
+            term = statics[WGT, c, here, :] * h
+            adj[TERM, c, here, :] = term
+            terms.append(term)
+        put_next(adj, 0, here, {TERM_R: terms})
+
+    sweep(forward_first, 0, chunks, G_FIRST)
     if rounds > 1:
         learn(1)
         if rounds > 2:
             tell(2)
-    sweep(functools.partial(forward_body, 1), 0, chunks, G_LAST)
+    sweep(forward_last, 0, chunks, G_LAST)
 
     def depth_body(i, carry):
         start = pl.multiple_of(i * 8, 8)
         for c in range(tiles):
             own = pl.ds(start + OWN, 8)
             depth_out[pl.ds(start, 8), c * LANES : (c + 1) * LANES] = jnp.where(
-                statics[WET, c, own, :] > 0.0, fields[2, H, c, own, :], raw_d[c, pl.ds(start, 8), :]
+                statics[WET, c, own, :] > 0.0, last_h[c, own, :], raw_d[c, pl.ds(start, 8), :]
             )
         return carry
 
@@ -582,69 +585,64 @@
         start = row + TOP
         here, after, before = pl.ds(start, 8), pl.ds(start + 1, 8), pl.ds(start - 1, 8)
 
-        def f_at(k, c, rows_at=here):
-            return fields[1, k, c, rows_at, :]
-
-        def p_at(k, c, rows_at=here):
-            return prims[1, k, c, rows_at, :]
-
-        def z_at(k, c, rows_at=here):
-            return adj[4, c, rows_at, :]
-
-        def one_face(h, n, u, cc, ih, z, inverse):
+        def one_face(coefs, lm, lp, h, n, z, p, r, ih):
+            alpha, beta, gamma = coefs[:3]
             gh = z[1] - z[0]
-            slopes = (gh * (n[1] - n[0]), gh * (h[1] - h[0]))
-            alpha, beta, gamma, left, right = speed_grads(u[0], cc[0], u[1], cc[1], inverse, slopes)
+            fast_l, slow_l, fast_r, slow_r = split_speed_grads(
+                *lm, *lp, coefs, gh * (n[1] - n[0]), gh * (h[1] - h[0])
+            )
             jump = gamma * gh
-            left_u, right_u = left[0] * ih[0], right[0] * ih[1]
             return (
-                0.5 * cc[0] * ih[0] * left[1] - left_u * u[0] - jump,
-                alpha * gh + left_u,
+                fast_l * p[0] - slow_l * r[0] - jump,
+                alpha * gh + (fast_l + slow_l) * ih[0],
             ), (
-                0.5 * cc[1] * ih[1] * right[1] - right_u * u[1] + jump,
-                beta * gh + right_u,
-            )
-
-        col_h, col_n, col_z = with_next(f_at, H), with_next(f_at, MY), with_next(z_at, 0)
-
-        def col_face(c):
-            u_r, c_r, ih_r = derived(col_h[c][1], col_n[c][1])
-            return one_face(
-                col_h[c], col_n[c], (p_at(UY, c), u_r), (p_at(CC, c), c_r), (p_at(IH, c), ih_r),
-                col_z[c], inverses[1, 1, c, here, :],
-            )
-
-        edge = col_face(wide - 1)
-        previous = edge
+                fast_r * p[1] - slow_r * r[1] + jump,
+                (fast_r + slow_r) * ih[1] - beta * gh,
+            )
+
+        lefts, rights = [], []
         for c in range(wide):
 
-            def pair(get, k):
-                return get(k, c), get(k, c, after)
+            def pair(k):
+                return s_at(k, c, here), s_right(k, c, here)
 
             left, right = one_face(
-                pair(f_at, H), pair(f_at, MX), pair(p_at, UX), pair(p_at, CC), pair(p_at, IH),
-                pair(z_at, 0), inverses[1, 0, c, here, :],
-            )
+                coefs_of(1, 1, c, here), pair(LMY), pair(LPY), pair(H), pair(MY),
+                (adj[TERM, c, here, :], adj[TERM_R, c, here, :]), pair(PY), pair(RY),
+                pair(IH),
+            )
+            lefts.append(left)
+            rights.append(right)
+        entering = [last_lanes([rights[c][k] for c in range(wide)]) for k in range(2)]
+        outs = []
+        for c in range(wide):
+
+            def pair(k):
+                return s_at(k, c, here), s_at(k, c, after)
+
+            left, right = one_face(
+                coefs_of(1, 0, c, here), pair(LMX), pair(LPX), pair(H), pair(MX),
+                (adj[TERM, c, here, :], adj[TERM, c, after, :]), pair(PX), pair(RX), pair(IH),
+            )
+            in_x = []
             for k in range(2):
-                shifted[k, c, here, :] = right[k]
-            in_x = [left[k] + shifted[k, c, before, :] for k in range(2)]
-            current = col_face(c) if c < wide - 1 else edge
-            in_y = [
-                current[0][k] + from_previous(current[1][k], previous[1][k]) for k in range(2)
-            ]
-            previous = current
-            adj_h = adj[3, c, here, :] + in_x[0] + in_y[0]
-            gain = TIME_RATIO * statics[WET, c, here, :]
-            adj[5, c, here, :] = adj_h
-            adj[0, c, here, :] = gain * adj_h
-            adj[1, c, here, :] = gain * in_x[1]
-            adj[2, c, here, :] = gain * in_y[1]
+                row_flux[k, c, here, :] = right[k]
+                in_x.append(left[k] + row_flux[k, c, before, :])
+            in_y = [lefts[c][k] + entering[k][c] for k in range(2)]
+            out = (adj[TERM, c, here, :] + (in_x[0] + in_y[0]), in_x[1], in_y[1])
+            for k, value in zip((ADJ, ZX, ZY), out):
+                adj[k, c, here, :] = value
+            outs.append(out)
+        put_next(
+            adj, 0, here,
+            {k: [outs[c][j] for c in range(wide)] for j, k in enumerate((ADJ_R, ZX_R, ZY_R))},
+        )
 
     sweep(backward_last, 0, chunks, G_BACK_LAST)
 
     own_hot = lax.broadcasted_iota(jnp.int32, (rows, dam_count), 0) == local_row
     gpart[...] = jnp.zeros(gpart.shape, jnp.float32)
-    for s, plane in ((0, 5), (1, 3)):
+    for s, plane in ((0, ADJ), (1, TERM)):
         picked = jnp.zeros((rows, dam_count), jnp.float32)
         for c in range(tiles):
             picked = picked + picked_by(
@@ -677,89 +675,69 @@
     for step in range(1, n_gy):
         gy_copy(step).start()
 
+    def first_face(coefs, lm, lp, h, n, t, q, v, zh, zn, zt, a, uv, p, r):
+        alpha, beta, gamma = coefs[:3]
+        gh, gn, gt = zh[1] - zh[0], zn[1] - zn[0], zt[1] - zt[0]
+        dn = n[1] - n[0]
+        fast_l, slow_l, fast_r, slow_r = split_speed_grads(
+            *lm, *lp, coefs,
+            gh * dn + gn * (q[1] - q[0]) + gt * (v[1] - v[0]),
+            gh * (h[1] - h[0]) + gn * dn + gt * (t[1] - t[0]),
+        )
+        jump = gamma * gh
+        return (
+            alpha * (gn * a[0] - gt * uv[0]) + (fast_l * p[0] - slow_l * r[0]) - jump,
+            (fast_r * p[1] - slow_r * r[1]) - beta * (gn * a[1] - gt * uv[1]) + jump,
+        )
+
+    def first_row_face(c, start):
+        here, after = pl.ds(start, 8), pl.ds(start + 1, 8)
+
+        def pair(k):
+            return f_at(k, c, here), f_at(k, c, after)
+
+        def z_pair(k):
+            return adj[k, c, here, :], adj[k, c, after, :]
+
+        return first_face(
+            coefs_of(0, 0, c, here), pair(LMX), pair(LPX), pair(H), pair(MX), pair(MY), pair(QX),
+            pair(TT), z_pair(ADJ), z_pair(ZX), z_pair(ZY), pair(AX), pair(UV), pair(PX), pair(RX),
+        )
+
+    for c in range(tiles):
+        row_flux[0, c, pl.ds(OWN - 8, 8), :] = first_row_face(c, OWN - 8)[1]
+
     def backward_first(row):
-        start = row + OWN - 8
-        out_row = max(row - 8, 0) if isinstance(row, int) else pl.multiple_of(jnp.maximum(row - 8, 0), 8)
-        here, after, before = pl.ds(start, 8), pl.ds(start + 1, 8), pl.ds(start - 1, 8)
-
-        def f_at(k, c, rows_at=here):
-            return fields[0, k, c, rows_at, :]
-
-        def p_at(k, c, rows_at=here):
-            return prims[0, k, c, rows_at, :]
-
-        def z_at(k, c, rows_at=here):
-            return adj[k, c, rows_at, :]
-
-        def one_face(h, n, t, u, cc, ih, q, v, zh, zn, zt, inverse):
-            gh, gn, gt = zh[1] - zh[0], zn[1] - zn[0], zt[1] - zt[0]
-            dn = n[1] - n[0]
-            slopes = (
-                gh * dn + gn * (q[1] - q[0]) + gt * (v[1] - v[0]),
-                gh * (h[1] - h[0]) + gn * dn + gt * (t[1] - t[0]),
-            )
-            alpha, beta, gamma, left, right = speed_grads(u[0], cc[0], u[1], cc[1], inverse, slopes)
-            jump = gamma * gh
-            out = []
-            for k, share, (g_u, g_c) in ((0, alpha, left), (1, beta, right)):
-                g_u = g_u + share * (gn * n[k] + gt * t[k])
-                rest = GRAVITY * h[k] * (share * gn) + ih[k] * (0.5 * cc[k] * g_c - g_u * u[k])
-                out.append(rest - jump if k == 0 else rest + jump)
-            return out
-
-        col_h, col_n, col_t = with_next(f_at, H), with_next(f_at, MY), with_next(f_at, MX)
-        col_zh, col_zn, col_zt = with_next(z_at, 0), with_next(z_at, 2), with_next(z_at, 1)
+        start = row + OWN
+        here, before = pl.ds(start, 8), pl.ds(start - 1, 8)
 
         def col_face(c):
-            h_r, n_r, t_r = col_h[c][1], col_n[c][1], col_t[c][1]
-            u_r, c_r, ih_r = derived(h_r, n_r)
-            q_r = n_r * u_r + (0.5 * GRAVITY) * h_r * h_r
-            return one_face(
-                col_h[c], col_n[c], col_t[c], (p_at(UY, c), u_r), (p_at(CC, c), c_r),
-                (p_at(IH, c), ih_r), (p_at(QY, c), q_r), (p_at(TT, c), t_r * u_r),
-                col_zh[c], col_zn[c], col_zt[c], inverses[0, 1, c, here, :],
-            )
-
-        previous = col_face(wide - 1)
+            def pair(k):
+                return f_at(k, c, here), f_right(k, c, here)
+
+            def z_pair(k):
+                return adj[k, c, here, :], adj[k + TERM_R - TERM, c, here, :]
+
+            return first_face(
+                coefs_of(0, 1, c, here), pair(LMY), pair(LPY), pair(H), pair(MY), pair(MX),
+                pair(QY), pair(TT), z_pair(ADJ), z_pair(ZY), z_pair(ZX), pair(AY), pair(UV),
+                pair(PY), pair(RY),
+            )
+
+        turned = pltpu.roll(col_face(wide - 1)[1], 1, 1)
         for c in range(tiles):
-
-            def pair(get, k):
-                return get(k, c), get(k, c, after)
-
-            left, right = one_face(
-                pair(f_at, H), pair(f_at, MX), pair(f_at, MY), pair(p_at, UX), pair(p_at, CC),
-                pair(p_at, IH), pair(p_at, QX), pair(p_at, TT), pair(z_at, 0), pair(z_at, 1),
-                pair(z_at, 2), inverses[0, 0, c, here, :],
-            )
-            shifted[0, c, here, :] = right
-            current = col_face(c)
-            across = left + shifted[0, c, before, :] + current[0]
-            across = across + from_previous(current[1], previous[1])
-            previous = current
-            h, mx, my = f_at(H, c), f_at(MX, c), f_at(MY, c)
-            ux, uy, ih = p_at(UX, c), p_at(UY, c), p_at(IH, c)
-            zx, zy = z_at(1, c), z_at(2, c)
-            normal_x = zx * statics[WDX, c, here, :]
-            normal_y = zy * statics[WDY, c, here, :]
-            wall_x = zx * statics[WSX, c, here, :] * mx
-            wall_y = zy * statics[WSY, c, here, :] * my
-
-            adjoint_out[pl.ds(out_row, 8), c * LANES : (c + 1) * LANES] = (
-                adj[5, c, here, :]
-                + across
-                - GRAVITY * h * (normal_x + normal_y)
-                + ih
-                * (
-                    normal_x * mx * ux
-                    + normal_y * my * uy
-                    + wall_x * jnp.abs(ux)
-                    + wall_y * jnp.abs(uy)
-                    - 0.5 * p_at(CC, c) * (wall_x + wall_y)
-                )
-            )
-
-    runs = rows // 8 + 1
-    half = runs // 2 // G_BACK_FIRST * G_BACK_FIRST
+            left, right = first_row_face(c, start)
+            row_flux[0, c, here, :] = right
+            left_y, right_y = col_face(c)
+            turned, last = pltpu.roll(right_y, 1, 1), turned
+            entering = jnp.where(lane == 0, last, turned)
+            across = left + row_flux[0, c, before, :] + (left_y + entering)
+            walls = adj[ZX, c, here, :] * f_at(BX, c, here) + adj[ZY, c, here, :] * f_at(BY, c, here)
+            adjoint_out[pl.ds(row, 8), c * LANES : (c + 1) * LANES] = (
+                adj[ADJ, c, here, :] + across - walls
+            )
+
+    half = rows // 16 // G_BACK_FIRST * G_BACK_FIRST
     sweep(backward_first, 0, half, G_BACK_FIRST)
 
     for step in range(1, n_gy):
@@ -775,7 +753,7 @@
     for step in range(1, n_gx):
         gx_copy(step).start()
 
-    sweep(backward_first, half, runs, G_BACK_FIRST)
+    sweep(backward_first, half, rows // 8, G_BACK_FIRST)
     for step in range(1, n_gx):
         gx_copy(step).wait()
     for step in range(1, n_gx):
@@ -821,12 +799,14 @@
             pltpu.VMEM(own, f32),
             pltpu.VMEM(own, jnp.int32),
             pltpu.VMEM(own, jnp.int32),
-            pltpu.VMEM((3, 3) + plane, f32),
-            pltpu.VMEM((2, 7) + plane, f32),
+            pltpu.VMEM((32,) + plane, f32),
+            pltpu.VMEM((19,) + plane, f32),
+            pltpu.VMEM((4,) + plane, f32),
+            pltpu.VMEM((2, 2, 7) + plane, f32),
+            pltpu.VMEM((2,) + plane, f32),
             pltpu.VMEM((8,) + plane, f32),
-            pltpu.VMEM((2, 2) + plane, f32),
-            pltpu.VMEM((2,) + plane, f32),
-            pltpu.VMEM((6,) + plane, f32),
+            pltpu.VMEM(plane, f32),
+            pltpu.VMEM((3,) + plane, f32),
             pltpu.VMEM((3,) + plane, f32),
             pltpu.VMEM((wide, LANES, dam_count), jnp.bfloat16),
             pltpu.VMEM((rows, LANES), f32),

time: 30 us -> 30.9 us (1.030)
  Pallas kernels: 27.2 us -> 28.1 us
    pallas_call x1, Pallas kernels: 27.2 us -> 28.1 us  [on_device(): pl.pallas_call(functools.partial(kernel, n_gx, n_gy, cols * n_gy, damage_...]
where the time goes in v2:
time: 30.9 us; the launch traced here: 30.7 us
  Pallas kernels  28.1 us (91%)
  local copies, waits for them, and re-layouts  1.97 us (6%)
  between operations  0.64 us (2%)
    pallas_call x1, Pallas kernels, on_device(): pl.pallas_call(functools.partial(kernel, n_gx, n_gy, cols * n_gy, damage_...  28.1 us
    unnamed x3, local copies, waits for them, and re-layouts  1.97 us

profile of v2, /device:TPU:0, one launch (start us, length us, event | category | flops | bytes accessed | tf_op | source)
XLA Modules:
  0.0 30.7 jit_solution(12999891998818833697)
XLA Ops:
  0.6 28.1 %window.1 = (f32[128,512]{1,0:T(8,128)S(1)}, f32[128,512]{1,0:T(8,128)S(1)}, f32[2,64]{1,0:T(2,128)S(1)}) custom-call(f32[128,512]{1,0:T(8,128)} %depth_in.1, f32[128,512]{1,0:T(8,128)} %mx_in.1, f32[128,512]{1,0:T(8,128)} %my_in.1, s32[128,512]{1,0:T(8,128)} %wet_in.1, s32[128,512]{1,0:T(8,128)} %class_in.1, f32[8]{0:T(128)} %rates_in.1, s32[1,64]{1,0:T(1,128)} %bitcast.5, ...), custom_call_target="tpu_custom_call" | custom-call | tf_op jit(solution)/shard_map/window/pallas_call | solution.py:787
  28.7 0.7 %copy.14 = f32[128,512]{1,0:T(8,128)} copy(f32[128,512]{1,0:T(8,128)S(1)} %get-tuple-element.9) | data formatting | bytes 524288
  29.4 0.6 %copy.16 = f32[64,2]{0,1:T(2,128)} copy(f32[64,2]{0,1:T(2,128)S(1)} %bitcast.3) | data formatting | bytes 1024
  30.0 0.7 %copy.15 = f32[128,512]{1,0:T(8,128)} copy(f32[128,512]{1,0:T(8,128)S(1)} %get-tuple-element.10) | data formatting | bytes 524288

commit v3 on v2

--- a/solution.py
+++ b/solution.py
@@ -14,7 +14,7 @@
 LANES = 128
 TOP = 8
 OWN = TOP + HALO
-G_STATIC, G_FIRST, G_LAST, G_BACK_LAST, G_BACK_FIRST = 2, 1, 2, 1, 1
+G_STATIC, G_FIRST, G_LAST, G_BACK_LAST, G_BACK_FIRST = 1, 1, 1, 1, 1
 MESH = pl.DeviceIdType.MESH
 
 
@@ -32,14 +32,37 @@
         body(8 * chunk)
 
 
-def picked_by(values, hot, dims):
-    out = None
+def pipeline(stages, first, last, group=1):
+    depth = len(stages)
+
+    def step(at, index=None):
+        for k in reversed(range(depth)):
+            if index is None or first <= index - k < last:
+                stages[k](at - 8 * k)
+
+    for index in range(first, first + depth - 1):
+        step(8 * index, index)
+    begin = first + depth - 1
+    whole = (last - begin) // group
+
+    def run(i, carry):
+        base = pl.multiple_of(i * (8 * group), 8)
+        for j in range(group):
+            step(base + 8 * (begin + j))
+        return carry
+
+    lax.fori_loop(0, whole, run, 0)
+    for index in range(begin + whole * group, last + depth - 1):
+        step(8 * index, index)
+
+
+def three_parts(values):
+    parts = []
     for _ in range(3):
         part = values.astype(jnp.bfloat16)
         values = values - part.astype(jnp.float32)
-        term = lax.dot_general(part, hot, (dims, ((), ())), preferred_element_type=jnp.float32)
-        out = term if out is None else out + term
-    return out
+        parts.append(part)
+    return parts
 
 
 def halved_on_tie(value, picks, ties):
@@ -293,12 +316,18 @@
     local_row = dam_row - ix * rows
     local_col = dam_col - iy * cols
     amounts = INFLOW_GAIN * releases[...]
-    wide_row = lax.broadcasted_iota(jnp.int32, (span, dam_count), 0) - HALO
-    row_hot = wide_row == local_row
+    thrice = lambda values: jnp.concatenate([values] * 3, axis=1)
+    amounts = jnp.concatenate(
+        [part.astype(jnp.float32) for part in three_parts(amounts)], axis=1
+    )
+    wide_row = lax.broadcasted_iota(jnp.int32, (span, 3 * dam_count), 0) - HALO
+    row_hot = wide_row == thrice(local_row)
     gain_rows = jnp.concatenate(
         [jnp.where(row_hot, amounts[s : s + 1], 0.0) for s in range(2)], axis=0
-    )
-    position = lax.broadcasted_iota(jnp.int32, (LANES, dam_count), 0)
+    ).astype(jnp.bfloat16)
+    position = lax.broadcasted_iota(jnp.int32, (LANES, 3 * dam_count), 0)
+    col_thrice = thrice(local_col)
+    hots = []
     for c in range(wide):
         if c < tiles:
             column = position + c * LANES
@@ -308,11 +337,19 @@
                 position + cols,
                 jnp.where(position >= LANES - HALO, position - LANES, -2 * LANES),
             )
-        hot = (column == local_col).astype(jnp.float32).astype(jnp.bfloat16)
-        col_hot[c] = hot
-        poured = picked_by(gain_rows, hot, ((1,), (1,)))
-        inflow[0, c, TOP : TOP + span, :] = poured[:span]
-        inflow[1, c, TOP : TOP + span, :] = poured[span:]
+        hot = (column == col_thrice).astype(jnp.float32).astype(jnp.bfloat16)
+        if c < tiles:
+            col_hot[c * LANES : (c + 1) * LANES, :] = hot[:, :dam_count]
+        hots.append(hot)
+    poured = lax.dot_general(
+        gain_rows, jnp.concatenate(hots, axis=0), (((1,), (1,)), ((), ())),
+        preferred_element_type=jnp.float32,
+    )
+    for s in range(2):
+        for c in range(wide):
+            inflow[s, c, TOP : TOP + span, :] = poured[
+                s * span : (s + 1) * span, c * LANES : (c + 1) * LANES
+            ]
 
     for index in range(8):
 
@@ -401,8 +438,9 @@
 
     FIRST_NEXT = (H, MX, MY, LMY, LPY, QY, TT, AY, UV, PY, RY)
     SECOND_NEXT = (H, MY, LMY, LPY, PY, RY, IH)
-
-    def base_prims(target, c, here, h, mx, my, ih):
+    SECOND_AT = 12
+
+    def base_prims(h, mx, my, ih):
         ux, uy = mx * ih, my * ih
         squared = GRAVITY * h
         cc = squared * lax.rsqrt(squared)
@@ -412,28 +450,36 @@
         out |= {PX: half_i - ux_i, RX: half_i + ux_i, PY: half_i - uy_i, RY: half_i + uy_i}
         return out, ux, uy, squared, cc, half
 
+    def static_shift(row):
+        here = pl.ds(row + TOP, 8)
+        wets = [statics[WET, c, here, :] for c in range(wide)]
+        for c, (right, left) in enumerate(zip(next_lanes(wets), last_lanes(wets))):
+            col_flux[0, c, here, :] = right
+            col_flux[1, c, here, :] = left
+        put_next(
+            first, NEXT, here,
+            {j: [first[k, c, here, :] for c in range(wide)] for j, k in enumerate((H, MX, MY))},
+        )
+
     def static_body(row):
         start = row + TOP
         here = pl.ds(start, 8)
-        wets = [statics[WET, c, here, :] for c in range(wide)]
-        rights, lefts = next_lanes(wets), last_lanes(wets)
-        kept = {k: [] for k in FIRST_NEXT}
         for c in range(wide):
-            wet = wets[c]
+            wet = statics[WET, c, here, :]
             above = statics[WET, c, pl.ds(start - 1, 8), :]
             below = statics[WET, c, pl.ds(start + 1, 8), :]
+            right, left = col_flux[0, c, here, :], col_flux[1, c, here, :]
             scale = TIME_RATIO * wet
             statics[FMX, c, here, :] = scale * below
-            statics[FMY, c, here, :] = scale * rights[c]
+            statics[FMY, c, here, :] = scale * right
             h, mx, my = (first[k, c, here, :] for k in (H, MX, MY))
-            ih = 1.0 / h
-            out, ux, uy, squared, cc, half = base_prims(first, c, here, h, mx, my, ih)
+            out, ux, uy, squared, cc, half = base_prims(h, mx, my, 1.0 / h)
             pressure = 0.5 * squared * h
             out[QX], out[QY], out[TT] = mx * ux + pressure, my * uy + pressure, mx * uy
             out[AX], out[AY], out[UV] = squared - ux * ux, squared - uy * uy, ux * uy
             for lower, upper, u, n, q, a, wall, back in (
                 (above, below, ux, mx, QX, AX, WX, BX),
-                (lefts[c], rights[c], uy, my, QY, AY, WY, BY),
+                (left, right, uy, my, QY, AY, WY, BY),
             ):
                 single = scale * (lower - upper)
                 both = scale * (2.0 - (lower + upper))
@@ -443,25 +489,27 @@
             for k, value in out.items():
                 if k not in (H, MX, MY):
                     first[k, c, here, :] = value
-            for k in FIRST_NEXT:
-                kept[k].append(out[k])
-        put_next(first, 0, here, {NEXT + j: kept[k] for j, k in enumerate(FIRST_NEXT)})
-
-    sweep(static_body, 0, chunks, G_STATIC)
-
-    def reader(source, keys):
+            h, mx, my = (first[NEXT + k, c, here, :] for k in range(3))
+            out, ux, uy, squared, cc, half = base_prims(h, mx, my, 1.0 / h)
+            out[QY], out[TT] = my * uy + 0.5 * squared * h, mx * uy
+            out[AY], out[UV] = squared - uy * uy, ux * uy
+            for j, k in enumerate(FIRST_NEXT):
+                if j >= 3:
+                    first[NEXT + j, c, here, :] = out[k]
+
+    pipeline((static_shift, static_body), 0, chunks, G_STATIC)
+
+    def reader(source, keys, offset):
         def at(k, c, rows_at):
             return source[k, c, rows_at, :]
 
         def right(k, c, rows_at):
-            return source[NEXT_OF[id(keys)] + keys.index(k), c, rows_at, :]
+            return source[offset + keys.index(k), c, rows_at, :]
 
         return at, right
 
-    SECOND_AT = 12
-    NEXT_OF = {id(FIRST_NEXT): NEXT, id(SECOND_NEXT): SECOND_AT}
-    f_at, f_right = reader(first, FIRST_NEXT)
-    s_at, s_right = reader(second, SECOND_NEXT)
+    f_at, f_right = reader(first, FIRST_NEXT, NEXT)
+    s_at, s_right = reader(second, SECOND_NEXT, SECOND_AT)
 
     def face(step, dim, c, here, lm_l, lm_r, lp_l, lp_r):
         low, high = jnp.minimum(lm_l, lm_r), jnp.maximum(lp_l, lp_r)
@@ -483,24 +531,27 @@
         alpha, beta, gamma = coefs
         return alpha * flux_l - beta * flux_r + gamma * (held_r - held_l)
 
-    def forward_first(row):
-        start = row + TOP
-        here, after, before = pl.ds(start, 8), pl.ds(start + 1, 8), pl.ds(start - 1, 8)
-        cols = []
+    def net_of(k, here):
+        values = [col_flux[k, c, here, :] for c in range(wide)]
+        return [mine - entering for mine, entering in zip(values, last_lanes(values))]
+
+    def first_cols(row):
+        here = pl.ds(row + TOP, 8)
         for c in range(wide):
             coefs = face(
                 0, 1, c, here, f_at(LMY, c, here), f_right(LMY, c, here),
                 f_at(LPY, c, here), f_right(LPY, c, here),
             )
-            cols.append([
-                crossing(
+            for k, (flux, held) in enumerate(((MY, H), (TT, MX), (QY, MY))):
+                col_flux[k, c, here, :] = crossing(
                     coefs, f_at(flux, c, here), f_right(flux, c, here),
                     f_at(held, c, here), f_right(held, c, here),
                 )
-                for flux, held in ((MY, H), (TT, MX), (QY, MY))
-            ])
-        entering = [last_lanes([cols[c][k] for c in range(wide)]) for k in range(3)]
-        kept = {k: [] for k in SECOND_NEXT}
+
+    def first_cells(row):
+        start = row + TOP
+        here, after, before = pl.ds(start, 8), pl.ds(start + 1, 8), pl.ds(start - 1, 8)
+        net = [net_of(k, here) for k in range(3)]
         for c in range(wide):
             coefs = face(
                 0, 0, c, here, f_at(LMX, c, here), f_at(LMX, c, after),
@@ -513,39 +564,46 @@
                     f_at(held, c, here), f_at(held, c, after),
                 )
                 row_flux[k, c, here, :] = value
-                change = value - row_flux[k, c, before, :] + (cols[c][k] - entering[k][c])
+                change = value - row_flux[k, c, before, :] + net[k][c]
                 if k > 0:
                     change = change + f_at((None, WX, WY)[k], c, here)
                 new.append(f_at((H, MX, MY)[k], c, here) - change)
             h = new[0] + inflow[0, c, here, :]
             ih = 1.0 / h
-            out = base_prims(second, c, here, h, new[1], new[2], ih)[0]
+            out = base_prims(h, new[1], new[2], ih)[0]
             out[IH] = ih
             for k, value in out.items():
                 second[k, c, here, :] = value
-            for k in SECOND_NEXT:
-                kept[k].append(out[k])
-        put_next(second, 0, here, {SECOND_AT + j: kept[k] for j, k in enumerate(SECOND_NEXT)})
+
+    def first_shift(row):
+        here = pl.ds(row + TOP, 8)
+        heights = next_lanes([second[H, c, here, :] for c in range(wide)])
+        flows = next_lanes([second[MY, c, here, :] for c in range(wide)])
+        for c, (h, n) in enumerate(zip(heights, flows)):
+            ih = 1.0 / h
+            out = base_prims(h, n, n, ih)[0]
+            out[IH] = ih
+            for j, k in enumerate(SECOND_NEXT):
+                second[SECOND_AT + j, c, here, :] = out[k]
 
     TERM, ADJ, ZX, ZY, TERM_R, ADJ_R, ZX_R, ZY_R = range(8)
 
-    def forward_last(row):
-        start = row + TOP
-        here, after, before = pl.ds(start, 8), pl.ds(start + 1, 8), pl.ds(start - 1, 8)
-        cols = []
+    def last_cols(row):
+        here = pl.ds(row + TOP, 8)
         for c in range(wide):
             coefs = face(
                 1, 1, c, here, s_at(LMY, c, here), s_right(LMY, c, here),
                 s_at(LPY, c, here), s_right(LPY, c, here),
             )
-            cols.append(
-                crossing(
-                    coefs, s_at(MY, c, here), s_right(MY, c, here),
-                    s_at(H, c, here), s_right(H, c, here),
-                )
-            )
-        entering = last_lanes(cols)
-        terms = []
+            col_flux[0, c, here, :] = crossing(
+                coefs, s_at(MY, c, here), s_right(MY, c, here),
+                s_at(H, c, here), s_right(H, c, here),
+            )
+
+    def last_cells(row):
+        start = row + TOP
+        here, after, before = pl.ds(start, 8), pl.ds(start + 1, 8), pl.ds(start - 1, 8)
+        net = net_of(0, here)
         for c in range(wide):
             coefs = face(
                 1, 0, c, here, s_at(LMX, c, here), s_at(LMX, c, after),
@@ -556,20 +614,25 @@
                 s_at(H, c, here), s_at(H, c, after),
             )
             row_flux[0, c, here, :] = value
-            change = value - row_flux[0, c, before, :] + (cols[c] - entering[c])
+            change = value - row_flux[0, c, before, :] + net[c]
             h = s_at(H, c, here) - change + inflow[1, c, here, :]
             last_h[c, here, :] = h
-            term = statics[WGT, c, here, :] * h
-            adj[TERM, c, here, :] = term
-            terms.append(term)
-        put_next(adj, 0, here, {TERM_R: terms})
-
-    sweep(forward_first, 0, chunks, G_FIRST)
+            adj[TERM, c, here, :] = statics[WGT, c, here, :] * h
+
+    def adj_shift(*planes):
+        def shift(row):
+            here = pl.ds(row + TOP, 8)
+            for k in planes:
+                put_next(adj, TERM_R + k, here, {0: [adj[k, c, here, :] for c in range(wide)]})
+
+        return shift
+
+    pipeline((first_cols, first_cells, first_shift), 0, chunks, G_FIRST)
     if rounds > 1:
         learn(1)
         if rounds > 2:
             tell(2)
-    sweep(forward_last, 0, chunks, G_LAST)
+    pipeline((last_cols, last_cells, adj_shift(TERM)), 0, chunks, G_LAST)
 
     def depth_body(i, carry):
         start = pl.multiple_of(i * 8, 8)
@@ -581,46 +644,48 @@
         return carry
 
     lax.fori_loop(0, rows // 8, depth_body, 0)
-    def backward_last(row):
+    def last_face(coefs, lm, lp, h, n, z, p, r, ih):
+        alpha, beta, gamma = coefs[:3]
+        gh = z[1] - z[0]
+        fast_l, slow_l, fast_r, slow_r = split_speed_grads(
+            *lm, *lp, coefs, gh * (n[1] - n[0]), gh * (h[1] - h[0])
+        )
+        jump = gamma * gh
+        return (
+            fast_l * p[0] - slow_l * r[0] - jump,
+            alpha * gh + (fast_l + slow_l) * ih[0],
+        ), (
+            fast_r * p[1] - slow_r * r[1] + jump,
+            (fast_r + slow_r) * ih[1] - beta * gh,
+        )
+
+    def back_cols(row):
+        here = pl.ds(row + TOP, 8)
+        for c in range(wide):
+
+            def pair(k):
+                return s_at(k, c, here), s_right(k, c, here)
+
+            left, right = last_face(
+                coefs_of(1, 1, c, here), pair(LMY), pair(LPY), pair(H), pair(MY),
+                (adj[TERM, c, here, :], adj[TERM_R, c, here, :]), pair(PY), pair(RY), pair(IH),
+            )
+            for k in range(2):
+                col_flux[k, c, here, :] = left[k]
+                col_flux[2 + k, c, here, :] = right[k]
+
+    def back_cells(row):
         start = row + TOP
         here, after, before = pl.ds(start, 8), pl.ds(start + 1, 8), pl.ds(start - 1, 8)
-
-        def one_face(coefs, lm, lp, h, n, z, p, r, ih):
-            alpha, beta, gamma = coefs[:3]
-            gh = z[1] - z[0]
-            fast_l, slow_l, fast_r, slow_r = split_speed_grads(
-                *lm, *lp, coefs, gh * (n[1] - n[0]), gh * (h[1] - h[0])
-            )
-            jump = gamma * gh
-            return (
-                fast_l * p[0] - slow_l * r[0] - jump,
-                alpha * gh + (fast_l + slow_l) * ih[0],
-            ), (
-                fast_r * p[1] - slow_r * r[1] + jump,
-                (fast_r + slow_r) * ih[1] - beta * gh,
-            )
-
-        lefts, rights = [], []
-        for c in range(wide):
-
-            def pair(k):
-                return s_at(k, c, here), s_right(k, c, here)
-
-            left, right = one_face(
-                coefs_of(1, 1, c, here), pair(LMY), pair(LPY), pair(H), pair(MY),
-                (adj[TERM, c, here, :], adj[TERM_R, c, here, :]), pair(PY), pair(RY),
-                pair(IH),
-            )
-            lefts.append(left)
-            rights.append(right)
-        entering = [last_lanes([rights[c][k] for c in range(wide)]) for k in range(2)]
-        outs = []
+        entering = [
+            last_lanes([col_flux[2 + k, c, here, :] for c in range(wide)]) for k in range(2)
+        ]
         for c in range(wide):
 
             def pair(k):
                 return s_at(k, c, here), s_at(k, c, after)
 
-            left, right = one_face(
+            left, right = last_face(
                 coefs_of(1, 0, c, here), pair(LMX), pair(LPX), pair(H), pair(MX),
                 (adj[TERM, c, here, :], adj[TERM, c, after, :]), pair(PX), pair(RX), pair(IH),
             )
@@ -628,28 +693,28 @@
             for k in range(2):
                 row_flux[k, c, here, :] = right[k]
                 in_x.append(left[k] + row_flux[k, c, before, :])
-            in_y = [lefts[c][k] + entering[k][c] for k in range(2)]
-            out = (adj[TERM, c, here, :] + (in_x[0] + in_y[0]), in_x[1], in_y[1])
-            for k, value in zip((ADJ, ZX, ZY), out):
-                adj[k, c, here, :] = value
-            outs.append(out)
-        put_next(
-            adj, 0, here,
-            {k: [outs[c][j] for c in range(wide)] for j, k in enumerate((ADJ_R, ZX_R, ZY_R))},
-        )
-
-    sweep(backward_last, 0, chunks, G_BACK_LAST)
+            in_y = [col_flux[k, c, here, :] + entering[k][c] for k in range(2)]
+            adj[ADJ, c, here, :] = adj[TERM, c, here, :] + (in_x[0] + in_y[0])
+            adj[ZX, c, here, :] = in_x[1]
+            adj[ZY, c, here, :] = in_y[1]
+
+    pipeline((back_cols, back_cells, adj_shift(ADJ, ZX, ZY)), 0, chunks, G_BACK_LAST)
 
     own_hot = lax.broadcasted_iota(jnp.int32, (rows, dam_count), 0) == local_row
     gpart[...] = jnp.zeros(gpart.shape, jnp.float32)
-    for s, plane in ((0, ADJ), (1, TERM)):
-        picked = jnp.zeros((rows, dam_count), jnp.float32)
-        for c in range(tiles):
-            picked = picked + picked_by(
-                adj[plane, c, OWN : OWN + rows, :], col_hot[c], ((1,), (0,))
-            )
+    stacked = []
+    for plane in (ADJ, TERM):
+        parts = [three_parts(adj[plane, c, OWN : OWN + rows, :]) for c in range(tiles)]
+        stacked.append(
+            jnp.concatenate([parts[c][k] for k in range(3) for c in range(tiles)], axis=1)
+        )
+    picked = lax.dot_general(
+        jnp.concatenate(stacked, axis=0), jnp.concatenate([col_hot[...]] * 3, axis=0),
+        (((1,), (0,)), ((), ())), preferred_element_type=jnp.float32,
+    )
+    for s in range(2):
         gpart[s : s + 1, 0:dam_count] = INFLOW_GAIN * jnp.sum(
-            jnp.where(own_hot, picked, 0.0), axis=0, keepdims=True
+            jnp.where(own_hot, picked[s * rows : (s + 1) * rows], 0.0), axis=0, keepdims=True
         )
 
     def gy_copy(step):
@@ -807,8 +872,8 @@
             pltpu.VMEM((8,) + plane, f32),
             pltpu.VMEM(plane, f32),
             pltpu.VMEM((3,) + plane, f32),
-            pltpu.VMEM((3,) + plane, f32),
-            pltpu.VMEM((wide, LANES, dam_count), jnp.bfloat16),
+            pltpu.VMEM((4,) + plane, f32),
+            pltpu.VMEM((cols, dam_count), jnp.bfloat16),
             pltpu.VMEM((rows, LANES), f32),
             pltpu.VMEM((2, tiles, 16, LANES), f32),
             pltpu.VMEM((2, tiles, 16, LANES), f32),

time: 30.9 us -> 27.6 us (0.89)
  Pallas kernels: 28.1 us -> 24.8 us
    pallas_call x1, Pallas kernels: 28.1 us -> 24.8 us  [on_device(): pl.pallas_call(functools.partial(kernel, n_gx, n_gy, cols * n_gy, damage_...]
where the time goes in v3:
time: 27.6 us; the launch traced here: 27.4 us
  Pallas kernels  24.8 us (90%)
  local copies, waits for them, and re-layouts  1.97 us (7%)
  between operations  0.64 us (2%)
    pallas_call x1, Pallas kernels, on_device(): pl.pallas_call(functools.partial(kernel, n_gx, n_gy, cols * n_gy, damage_...  24.8 us
    unnamed x3, local copies, waits for them, and re-layouts  1.97 us

profile of v3, /device:TPU:0, one launch (start us, length us, event | category | flops | bytes accessed | tf_op | source)
XLA Modules:
  0.0 27.4 jit_solution(8191936576021629635)
XLA Ops:
  0.6 24.8 %window.1 = (f32[128,512]{1,0:T(8,128)S(1)}, f32[128,512]{1,0:T(8,128)S(1)}, f32[2,64]{1,0:T(2,128)S(1)}) custom-call(f32[128,512]{1,0:T(8,128)} %depth_in.1, f32[128,512]{1,0:T(8,128)} %mx_in.1, f32[128,512]{1,0:T(8,128)} %my_in.1, s32[128,512]{1,0:T(8,128)} %wet_in.1, s32[128,512]{1,0:T(8,128)} %class_in.1, f32[8]{0:T(128)} %rates_in.1, s32[1,64]{1,0:T(1,128)} %bitcast.5, ...), custom_call_target="tpu_custom_call" | custom-call | tf_op jit(solution)/shard_map/window/pallas_call | solution.py:852
  25.4 0.7 %copy.14 = f32[128,512]{1,0:T(8,128)} copy(f32[128,512]{1,0:T(8,128)S(1)} %get-tuple-element.9) | data formatting | bytes 524288
  26.1 0.6 %copy.16 = f32[64,2]{0,1:T(2,128)} copy(f32[64,2]{0,1:T(2,128)S(1)} %bitcast.3) | data formatting | bytes 1024
  26.7 0.7 %copy.15 = f32[128,512]{1,0:T(8,128)} copy(f32[128,512]{1,0:T(8,128)S(1)} %get-tuple-element.10) | data formatting | bytes 524288

commit v4 on v3

--- a/solution.py
+++ b/solution.py
@@ -14,7 +14,7 @@
 LANES = 128
 TOP = 8
 OWN = TOP + HALO
-G_STATIC, G_FIRST, G_LAST, G_BACK_LAST, G_BACK_FIRST = 1, 1, 1, 1, 1
+G_STATIC, G_FIRST, G_LAST, G_BACK_LAST, G_BACK_FIRST = 3, 3, 5, 3, 1
 MESH = pl.DeviceIdType.MESH
 
 
@@ -116,9 +116,7 @@
     recv_cols,
     recv_corner,
     gpart,
-    gsum,
-    recv_gy,
-    recv_gx,
+    recv_all,
     rates,
     dams,
     releases,
@@ -127,10 +125,8 @@
     in_sem,
     edge_send,
     edge_recv,
-    gy_send,
-    gy_recv,
-    gx_send,
-    gx_recv,
+    grad_send,
+    grad_recv,
 ):
     rows, cols = depth_in.shape
     tiles = cols // LANES
@@ -233,7 +229,7 @@
 
     pl.semaphore_wait(barrier, (n_gy - 1) + corners)
 
-    rounds = max(n_gx - 2, 0).bit_length()
+    rounds = (n_gx - 1).bit_length()
 
     def reach(level):
         return (ix >= 2**level, -(2**level)), (ix + 2**level < n_gx, 2**level)
@@ -701,7 +697,6 @@
     pipeline((back_cols, back_cells, adj_shift(ADJ, ZX, ZY)), 0, chunks, G_BACK_LAST)
 
     own_hot = lax.broadcasted_iota(jnp.int32, (rows, dam_count), 0) == local_row
-    gpart[...] = jnp.zeros(gpart.shape, jnp.float32)
     stacked = []
     for plane in (ADJ, TERM):
         parts = [three_parts(adj[plane, c, OWN : OWN + rows, :]) for c in range(tiles)]
@@ -712,33 +707,36 @@
         jnp.concatenate(stacked, axis=0), jnp.concatenate([col_hot[...]] * 3, axis=0),
         (((1,), (0,)), ((), ())), preferred_element_type=jnp.float32,
     )
-    for s in range(2):
-        gpart[s : s + 1, 0:dam_count] = INFLOW_GAIN * jnp.sum(
-            jnp.where(own_hot, picked[s * rows : (s + 1) * rows], 0.0), axis=0, keepdims=True
-        )
-
-    def gy_copy(step):
-        return pltpu.make_async_remote_copy(
+    gpart[...] = jnp.concatenate(
+        [
+            INFLOW_GAIN * jnp.sum(
+                jnp.where(own_hot, picked[s * rows : (s + 1) * rows], 0.0), axis=0, keepdims=True
+            )
+            for s in range(2)
+        ],
+        axis=1,
+    )
+
+    for level in range(2, rounds):
+        learn(level)
+        if level + 1 < rounds:
+            tell(level + 1)
+
+    count = n_gx * n_gy
+
+    def send_grads(k, carry):
+        to = lax.rem(ix * n_gy + iy + 1 + k, count)
+        pltpu.make_async_remote_copy(
             src_ref=gpart,
-            dst_ref=recv_gy.at[step - 1],
-            send_sem=gy_send.at[step - 1],
-            recv_sem=gy_recv.at[step - 1],
-            device_id=(ix, lax.rem(iy + step, n_gy)),
+            dst_ref=recv_all.at[k],
+            send_sem=grad_send.at[0],
+            recv_sem=grad_recv.at[0],
+            device_id=(lax.div(to, n_gy), lax.rem(to, n_gy)),
             device_id_type=MESH,
-        )
-
-    def gx_copy(step):
-        return pltpu.make_async_remote_copy(
-            src_ref=gsum,
-            dst_ref=recv_gx.at[step - 1],
-            send_sem=gx_send.at[step - 1],
-            recv_sem=gx_recv.at[step - 1],
-            device_id=(lax.rem(ix + step, n_gx), iy),
-            device_id_type=MESH,
-        )
-
-    for step in range(1, n_gy):
-        gy_copy(step).start()
+        ).start()
+        return carry
+
+    lax.fori_loop(0, count - 1, send_grads, 0)
 
     def first_face(coefs, lm, lp, h, n, t, q, v, zh, zn, zt, a, uv, p, r):
         alpha, beta, gamma = coefs[:3]
@@ -802,28 +800,13 @@
                 adj[ADJ, c, here, :] + across - walls
             )
 
-    half = rows // 16 // G_BACK_FIRST * G_BACK_FIRST
-    sweep(backward_first, 0, half, G_BACK_FIRST)
-
-    for step in range(1, n_gy):
-        gy_copy(step).wait()
-    total = gpart[...]
-    for step in range(1, n_gy):
-        total = total + recv_gy[step - 1]
-    gsum[...] = total
-    for level in range(2, rounds):
-        learn(level)
-        if level + 1 < rounds:
-            tell(level + 1)
-    for step in range(1, n_gx):
-        gx_copy(step).start()
-
-    sweep(backward_first, half, rows // 8, G_BACK_FIRST)
-    for step in range(1, n_gx):
-        gx_copy(step).wait()
-    for step in range(1, n_gx):
-        total = total + recv_gx[step - 1]
-    grad_out[...] = total[0:2, 0:dam_count]
+    sweep(backward_first, 0, rows // 8, G_BACK_FIRST)
+
+    for sem in (grad_send, grad_recv):
+        pltpu.make_async_copy(recv_all, recv_all, sem.at[0]).wait()
+    total = gpart[...] + jnp.sum(recv_all[...], axis=0)
+    for s in range(2):
+        grad_out[s : s + 1, :] = total[:, s * dam_count : (s + 1) * dam_count]
 
 
 def on_device(
@@ -880,22 +863,18 @@
             pltpu.VMEM((2, 16, rows), f32),
             pltpu.VMEM((2, 16, rows), f32),
             pltpu.VMEM((4, 8, LANES), f32),
-            pltpu.VMEM((8, LANES), f32),
-            pltpu.VMEM((8, LANES), f32),
-            pltpu.VMEM((n_gy - 1, 8, LANES), f32),
-            pltpu.VMEM((n_gx - 1, 8, LANES), f32),
+            pltpu.VMEM((1, 2 * dam_count), f32),
+            pltpu.VMEM((n_gx * n_gy - 1, 1, 2 * dam_count), f32),
             pltpu.SMEM(damage_rates.shape, f32),
             pltpu.VMEM((1, dam_count), jnp.int32),
             pltpu.VMEM(releases.shape[::-1], f32),
             dma((3,)),
-            pltpu.SemaphoreType.REGULAR((max(n_gx - 2, 1).bit_length(),)),
+            pltpu.SemaphoreType.REGULAR((max((n_gx - 1).bit_length(), 1),)),
             dma((5, tiles)),
             dma((8,)),
             dma((8,)),
-            dma((n_gy - 1,)),
-            dma((n_gy - 1,)),
-            dma((n_gx - 1,)),
-            dma((n_gx - 1,)),
+            dma((1,)),
+            dma((1,)),
         ],
         compiler_params=pltpu.CompilerParams(
             collective_id=0, has_side_effects=True, vmem_limit_bytes=56 * 1024 * 1024

time: 27.6 us -> 24.2 us (0.88)
  Pallas kernels: 24.8 us -> 21.4 us
    pallas_call x1, Pallas kernels: 24.8 us -> 21.4 us  [on_device(): pl.pallas_call(functools.partial(kernel, n_gx, n_gy, cols * n_gy, damage_...]
where the time goes in v4:
time: 24.2 us; the launch traced here: 24 us
  Pallas kernels  21.4 us (88%)
  local copies, waits for them, and re-layouts  1.97 us (8%)
  between operations  0.64 us (3%)
    pallas_call x1, Pallas kernels, on_device(): pl.pallas_call(functools.partial(kernel, n_gx, n_gy, cols * n_gy, damage_...  21.4 us
    unnamed x3, local copies, waits for them, and re-layouts  1.97 us

profile of v4, /device:TPU:0, one launch (start us, length us, event | category | flops | bytes accessed | tf_op | source)
XLA Modules:
  0.0 24.0 jit_solution(4092651352646158557)
XLA Ops:
  0.6 21.4 %window.1 = (f32[128,512]{1,0:T(8,128)S(1)}, f32[128,512]{1,0:T(8,128)S(1)}, f32[2,64]{1,0:T(2,128)S(1)}) custom-call(f32[128,512]{1,0:T(8,128)} %depth_in.1, f32[128,512]{1,0:T(8,128)} %mx_in.1, f32[128,512]{1,0:T(8,128)} %my_in.1, s32[128,512]{1,0:T(8,128)} %wet_in.1, s32[128,512]{1,0:T(8,128)} %class_in.1, f32[8]{0:T(128)} %rates_in.1, s32[1,64]{1,0:T(1,128)} %bitcast.5, ...), custom_call_target="tpu_custom_call" | custom-call | tf_op jit(solution)/shard_map/window/pallas_call | solution.py:835
  22.0 0.7 %copy.14 = f32[128,512]{1,0:T(8,128)} copy(f32[128,512]{1,0:T(8,128)S(1)} %get-tuple-element.9) | data formatting | bytes 524288
  22.7 0.6 %copy.16 = f32[64,2]{0,1:T(2,128)} copy(f32[64,2]{0,1:T(2,128)S(1)} %bitcast.3) | data formatting | bytes 1024
  23.3 0.7 %copy.15 = f32[128,512]{1,0:T(8,128)} copy(f32[128,512]{1,0:T(8,128)S(1)} %get-tuple-element.10) | data formatting | bytes 524288

commit v5 on v4

--- a/solution.py
+++ b/solution.py
@@ -809,6 +809,18 @@
         grad_out[s : s + 1, :] = total[:, s * dam_count : (s + 1) * dam_count]
 
 
+def place(*refs):
+    sources, targets, sem = refs[:3], refs[3:6], refs[6]
+    copies = [
+        pltpu.make_async_copy(source, target, sem.at[k])
+        for k, (source, target) in enumerate(zip(sources, targets))
+    ]
+    for copy in copies:
+        copy.start()
+    for copy in copies:
+        copy.wait()
+
+
 def on_device(
     n_gx,
     n_gy,
@@ -832,7 +844,7 @@
     anywhere = pl.BlockSpec(memory_space=pl.ANY)
     vmem = pl.BlockSpec(memory_space=pltpu.VMEM)
     dma = pltpu.SemaphoreType.DMA
-    final_depth, adjoint, grad = pl.pallas_call(
+    results = pl.pallas_call(
         functools.partial(kernel, n_gx, n_gy, cols * n_gy, damage_rates.shape[0]),
         out_shape=(
             pltpu.VMEM((rows, cols), f32),
@@ -890,6 +902,14 @@
         dam_cell.reshape(1, dam_count),
         releases.T,
     )
+    final_depth, adjoint, grad = pl.pallas_call(
+        place,
+        out_shape=tuple(jax.ShapeDtypeStruct(value.shape, f32) for value in results),
+        in_specs=[vmem] * 3,
+        out_specs=(anywhere,) * 3,
+        scratch_shapes=[dma((3,))],
+        name="place",
+    )(*(pltpu.with_memory_space_constraint(value, pltpu.VMEM) for value in results))
     return final_depth, adjoint, grad.T
 
 

time: 24.2 us -> 23 us (0.950)
  local copies, waits for them, and re-layouts: 1.97 us -> 0 us
  Pallas kernels: 21.4 us -> 22.2 us
    unnamed x3 -> x0, local copies, waits for them, and re-layouts: 1.97 us -> none
    pallas_call x0 -> x1, Pallas kernels: none -> 0.82 us  [on_device(): pl.pallas_call(place, out_shape=tuple((jax.ShapeDtypeStruct(value.shape,...]
where the time goes in v5:
time: 23 us; the launch traced here: 22.9 us
  Pallas kernels  22.2 us (97%)
  between operations  0.64 us (3%)
    pallas_call x1, Pallas kernels, on_device(): pl.pallas_call(functools.partial(kernel, n_gx, n_gy, cols * n_gy, damage_...  21.4 us
    pallas_call x1, Pallas kernels, on_device(): pl.pallas_call(place, out_shape=tuple((jax.ShapeDtypeStruct(value.shape,...  0.82 us

profile of v5, /device:TPU:0, one launch (start us, length us, event | category | flops | bytes accessed | tf_op | source)
XLA Modules:
  0.0 22.9 jit_solution(4339363285291633388)
XLA Ops:
  0.6 21.4 %window.1 = (f32[128,512]{1,0:T(8,128)S(1)}, f32[128,512]{1,0:T(8,128)S(1)}, f32[2,64]{1,0:T(2,128)S(1)}) custom-call(f32[128,512]{1,0:T(8,128)} %depth_in.1, f32[128,512]{1,0:T(8,128)} %mx_in.1, f32[128,512]{1,0:T(8,128)} %my_in.1, s32[128,512]{1,0:T(8,128)} %wet_in.1, s32[128,512]{1,0:T(8,128)} %class_in.1, f32[8]{0:T(128)} %rates_in.1, s32[1,64]{1,0:T(1,128)} %bitcast.4, ...), custom_call_target="tpu_custom_call" | custom-call | tf_op jit(solution)/shard_map/window/pallas_call | solution.py:847
  22.0 0.8 %place.1 = (f32[128,512]{1,0:T(8,128)}, f32[128,512]{1,0:T(8,128)}, f32[2,64]{1,0:T(2,128)}) custom-call(f32[128,512]{1,0:T(8,128)S(1)} %get-tuple-element.9.refs_0_, f32[128,512]{1,0:T(8,128)S(1)} %get-tuple-element.10.refs_1_, f32[2,64]{1,0:T(2,128)S(1)} %get-tuple-element.11.refs_2_), custom_call_target="tpu_custom_call" | custom-call | tf_op jit(solution)/shard_map/place/pallas_call | solution.py:905

commit v6 on v5

--- a/solution.py
+++ b/solution.py
@@ -14,7 +14,7 @@
 LANES = 128
 TOP = 8
 OWN = TOP + HALO
-G_STATIC, G_FIRST, G_LAST, G_BACK_LAST, G_BACK_FIRST = 3, 3, 5, 3, 1
+G_STATIC, G_FACES, G_OUTER, G_FIRST, G_LAST, G_BACK_LAST, G_BACK_FIRST = 2, 2, 2, 3, 5, 3, 1
 MESH = pl.DeviceIdType.MESH
 
 
@@ -32,18 +32,21 @@
         body(8 * chunk)
 
 
-def pipeline(stages, first, last, group=1):
+def pipeline(stages, first, last, group=1, begin=None, end=None):
     depth = len(stages)
+    begin = first + depth - 1 if begin is None else begin
+    end = last if end is None else end
 
     def step(at, index=None):
         for k in reversed(range(depth)):
-            if index is None or first <= index - k < last:
-                stages[k](at - 8 * k)
-
-    for index in range(first, first + depth - 1):
+            if index is None:
+                stages[k](at - 8 * k, None)
+            elif first <= index - k < last:
+                stages[k](at - 8 * k, index - k)
+
+    for index in range(first, begin):
         step(8 * index, index)
-    begin = first + depth - 1
-    whole = (last - begin) // group
+    whole = (end - begin) // group
 
     def run(i, carry):
         base = pl.multiple_of(i * (8 * group), 8)
@@ -347,6 +350,186 @@
                 s * span : (s + 1) * span, c * LANES : (c + 1) * LANES
             ]
 
+    def turned(get, cs, shift, step):
+        needed = sorted({c for c in cs} | {(c + step) % wide for c in cs})
+        values = {c: pltpu.roll(get(c), shift, 1) for c in needed}
+        edge = LANES - 1 if step > 0 else 0
+        return {c: jnp.where(lane == edge, values[(c + step) % wide], values[c]) for c in cs}
+
+    def next_lanes(values, cs=None):
+        cs = range(wide) if cs is None else cs
+        return list(turned(lambda c: values[c], cs, LANES - 1, 1).values())
+
+    def last_lanes(values):
+        return list(turned(lambda c: values[c], range(wide), 1, -1).values())
+
+    FIRST_NEXT = (H, MX, MY, LMY, LPY, QY, TT, AY, UV, PY, RY)
+    SECOND_NEXT = (H, MY, LMY, LPY, PY, RY, IH)
+    SECOND_AT = 12
+
+    def base_prims(h, mx, my, ih):
+        ux, uy = mx * ih, my * ih
+        squared = GRAVITY * h
+        cc = squared * lax.rsqrt(squared)
+        half = 0.5 * cc
+        out = {H: h, MX: mx, MY: my, LMX: ux - cc, LPX: ux + cc, LMY: uy - cc, LPY: uy + cc}
+        half_i, ux_i, uy_i = half * ih, ux * ih, uy * ih
+        out |= {PX: half_i - ux_i, RX: half_i + ux_i, PY: half_i - uy_i, RY: half_i + uy_i}
+        return out, ux, uy, squared, cc, half
+
+    def reader(source, keys, offset):
+        def at(k, c, rows_at):
+            return source[k, c, rows_at, :]
+
+        def right(k, c, rows_at):
+            return source[offset + keys.index(k), c, rows_at, :]
+
+        return at, right
+
+    f_at, f_right = reader(first, FIRST_NEXT, NEXT)
+    s_at, s_right = reader(second, SECOND_NEXT, SECOND_AT)
+
+    def face(step, dim, c, here, lm_l, lm_r, lp_l, lp_r):
+        low, high = jnp.minimum(lm_l, lm_r), jnp.maximum(lp_l, lp_r)
+        slow, fast = jnp.minimum(low, 0.0), jnp.maximum(high, 0.0)
+        inverse = 1.0 / (fast - slow)
+        masked = statics[FMX + dim, c, here, :] * inverse
+        alpha, beta = fast * masked, slow * masked
+        gamma = slow * alpha
+        e_slow = halved_on_tie(alpha * inverse, low < 0.0, low == 0.0)
+        e_fast = halved_on_tie(beta * inverse, high > 0.0, high == 0.0)
+        for k, value in enumerate((alpha, beta, gamma, slow, fast, e_slow, e_fast)):
+            faces[step, dim, k, c, here, :] = value
+        return alpha, beta, gamma
+
+    def coefs_of(step, dim, c, here):
+        return [faces[step, dim, k, c, here, :] for k in range(7)]
+
+    def crossing(coefs, flux_l, flux_r, held_l, held_r):
+        alpha, beta, gamma = coefs
+        return alpha * flux_l - beta * flux_r + gamma * (held_r - held_l)
+
+    def net_of(k, here):
+        values = [col_flux[k, c, here, :] for c in range(wide)]
+        return [mine - entering for mine, entering in zip(values, last_lanes(values))]
+
+    RIGHT, LEFT = 0, 1
+    EVERY = tuple(range(wide))
+
+    def shift_stage(rights, lefts):
+        def shift(row):
+            here = pl.ds(row + TOP, 8)
+
+            def wet_at(c):
+                return statics[WET, c, here, :]
+
+            for c, value in turned(wet_at, rights, LANES - 1, 1).items():
+                adj[RIGHT, c, here, :] = value
+            for c, value in turned(wet_at, lefts, 1, -1).items():
+                adj[LEFT, c, here, :] = value
+            for j, k in enumerate((H, MX, MY)):
+                shifted = turned(lambda c, k=k: first[k, c, here, :], rights, LANES - 1, 1)
+                for c, value in shifted.items():
+                    first[NEXT + j, c, here, :] = value
+
+        return shift
+
+    def walls_of(scale, lower, upper, u, n, q, a, cc, half):
+        single = scale * (lower - upper)
+        both = scale * (2.0 - (lower + upper))
+        size = jnp.abs(u)
+        return single * q + both * ((size + cc) * n), single * a + both * (u * (half - size))
+
+    def static_x(c, start):
+        here = pl.ds(start, 8)
+        scale = TIME_RATIO * statics[WET, c, here, :]
+        above = statics[WET, c, pl.ds(start - 1, 8), :]
+        below = statics[WET, c, pl.ds(start + 1, 8), :]
+        statics[FMX, c, here, :] = scale * below
+        h, mx, my = (first[k, c, here, :] for k in (H, MX, MY))
+        out, ux, uy, squared, cc, half = base_prims(h, mx, my, 1.0 / h)
+        pressure = 0.5 * squared * h
+        out[QX], out[QY], out[TT] = mx * ux + pressure, my * uy + pressure, mx * uy
+        out[AX], out[AY], out[UV] = squared - ux * ux, squared - uy * uy, ux * uy
+        out[WX], out[BX] = walls_of(scale, above, below, ux, mx, out[QX], out[AX], cc, half)
+        for k, value in out.items():
+            if k not in (H, MX, MY):
+                first[k, c, here, :] = value
+        return uy, my, out[QY], out[AY], cc, half
+
+    def static_y(c, here, parts=None):
+        scale = TIME_RATIO * statics[WET, c, here, :]
+        if parts is None:
+            h, my = first[H, c, here, :], first[MY, c, here, :]
+            squared = GRAVITY * h
+            cc = squared * lax.rsqrt(squared)
+            parts = my * (1.0 / h), my, first[QY, c, here, :], first[AY, c, here, :], cc, 0.5 * cc
+        first[WY, c, here, :], first[BY, c, here, :] = walls_of(
+            scale, adj[LEFT, c, here, :], adj[RIGHT, c, here, :], *parts
+        )
+
+    def static_next(c, here):
+        scale = TIME_RATIO * statics[WET, c, here, :]
+        statics[FMY, c, here, :] = scale * adj[RIGHT, c, here, :]
+        h, mx, my = (first[NEXT + k, c, here, :] for k in range(3))
+        out, ux, uy, squared, cc, half = base_prims(h, mx, my, 1.0 / h)
+        out[QY], out[TT] = my * uy + 0.5 * squared * h, mx * uy
+        out[AY], out[UV] = squared - uy * uy, ux * uy
+        for j, k in enumerate(FIRST_NEXT):
+            if j >= 3:
+                first[NEXT + j, c, here, :] = out[k]
+
+    def static_stage(xs, ys, nexts):
+        def static(row):
+            start = row + TOP
+            here = pl.ds(start, 8)
+            for c in range(wide):
+                parts = static_x(c, start) if c in xs else None
+                if c in ys:
+                    static_y(c, here, parts)
+                if c in nexts:
+                    static_next(c, here)
+
+        return static
+
+    def first_faces(cols_at, rows_at):
+        def faces_of(row):
+            start = row + TOP
+            here, after = pl.ds(start, 8), pl.ds(start + 1, 8)
+            for c in cols_at:
+                coefs = face(
+                    0, 1, c, here, f_at(LMY, c, here), f_right(LMY, c, here),
+                    f_at(LPY, c, here), f_right(LPY, c, here),
+                )
+                for k, (flux, held) in enumerate(((MY, H), (TT, MX), (QY, MY))):
+                    col_flux[k, c, here, :] = crossing(
+                        coefs, f_at(flux, c, here), f_right(flux, c, here),
+                        f_at(held, c, here), f_right(held, c, here),
+                    )
+            for c in rows_at:
+                coefs = face(
+                    0, 0, c, here, f_at(LMX, c, here), f_at(LMX, c, after),
+                    f_at(LPX, c, here), f_at(LPX, c, after),
+                )
+                for k, (flux, held) in enumerate(((MX, H), (QX, MX), (TT, MY))):
+                    row_flux[k, c, here, :] = crossing(
+                        coefs, f_at(flux, c, here), f_at(flux, c, after),
+                        f_at(held, c, here), f_at(held, c, after),
+                    )
+
+        return faces_of
+
+    inner, own_tiles = EVERY[: tiles - 1], EVERY[:tiles]
+    shift_inner = shift_stage(inner, EVERY[1:tiles])
+    static_inner = static_stage(own_tiles, EVERY[1 : tiles - 1], inner)
+    faces_inner = first_faces(inner, own_tiles)
+
+    def plain(stage):
+        return lambda row, index: stage(row)
+
+    pipeline((plain(shift_inner), plain(static_inner)), 1, chunks - 1, G_STATIC)
+    pipeline((plain(faces_inner),), 1, chunks - 2, G_FACES)
+
     for index in range(8):
 
         @pl.when(sides[index][0])
@@ -414,152 +597,34 @@
         ]
         put_start(tiles, at_rows, 4, four)
 
-    def next_lanes(values):
-        turned_all = [pltpu.roll(value, LANES - 1, 1) for value in values]
-        return [
-            jnp.where(lane == LANES - 1, turned_all[(c + 1) % wide], turned_all[c])
-            for c in range(wide)
-        ]
-
-    def last_lanes(values):
-        turned_all = [pltpu.roll(value, 1, 1) for value in values]
-        return [
-            jnp.where(lane == 0, turned_all[(c - 1) % wide], turned_all[c]) for c in range(wide)
-        ]
-
-    def put_next(target, offset, here, columns):
-        for k, values in columns.items():
-            for c, value in enumerate(next_lanes(values)):
-                target[offset + k, c, here, :] = value
-
-    FIRST_NEXT = (H, MX, MY, LMY, LPY, QY, TT, AY, UV, PY, RY)
-    SECOND_NEXT = (H, MY, LMY, LPY, PY, RY, IH)
-    SECOND_AT = 12
-
-    def base_prims(h, mx, my, ih):
-        ux, uy = mx * ih, my * ih
-        squared = GRAVITY * h
-        cc = squared * lax.rsqrt(squared)
-        half = 0.5 * cc
-        out = {H: h, MX: mx, MY: my, LMX: ux - cc, LPX: ux + cc, LMY: uy - cc, LPY: uy + cc}
-        half_i, ux_i, uy_i = half * ih, ux * ih, uy * ih
-        out |= {PX: half_i - ux_i, RX: half_i + ux_i, PY: half_i - uy_i, RY: half_i + uy_i}
-        return out, ux, uy, squared, cc, half
-
-    def static_shift(row):
-        here = pl.ds(row + TOP, 8)
-        wets = [statics[WET, c, here, :] for c in range(wide)]
-        for c, (right, left) in enumerate(zip(next_lanes(wets), last_lanes(wets))):
-            col_flux[0, c, here, :] = right
-            col_flux[1, c, here, :] = left
-        put_next(
-            first, NEXT, here,
-            {j: [first[k, c, here, :] for c in range(wide)] for j, k in enumerate((H, MX, MY))},
-        )
-
-    def static_body(row):
-        start = row + TOP
-        here = pl.ds(start, 8)
-        for c in range(wide):
-            wet = statics[WET, c, here, :]
-            above = statics[WET, c, pl.ds(start - 1, 8), :]
-            below = statics[WET, c, pl.ds(start + 1, 8), :]
-            right, left = col_flux[0, c, here, :], col_flux[1, c, here, :]
-            scale = TIME_RATIO * wet
-            statics[FMX, c, here, :] = scale * below
-            statics[FMY, c, here, :] = scale * right
-            h, mx, my = (first[k, c, here, :] for k in (H, MX, MY))
-            out, ux, uy, squared, cc, half = base_prims(h, mx, my, 1.0 / h)
-            pressure = 0.5 * squared * h
-            out[QX], out[QY], out[TT] = mx * ux + pressure, my * uy + pressure, mx * uy
-            out[AX], out[AY], out[UV] = squared - ux * ux, squared - uy * uy, ux * uy
-            for lower, upper, u, n, q, a, wall, back in (
-                (above, below, ux, mx, QX, AX, WX, BX),
-                (left, right, uy, my, QY, AY, WY, BY),
-            ):
-                single = scale * (lower - upper)
-                both = scale * (2.0 - (lower + upper))
-                size = jnp.abs(u)
-                out[wall] = single * out[q] + both * ((size + cc) * n)
-                out[back] = single * out[a] + both * (u * (half - size))
-            for k, value in out.items():
-                if k not in (H, MX, MY):
-                    first[k, c, here, :] = value
-            h, mx, my = (first[NEXT + k, c, here, :] for k in range(3))
-            out, ux, uy, squared, cc, half = base_prims(h, mx, my, 1.0 / h)
-            out[QY], out[TT] = my * uy + 0.5 * squared * h, mx * uy
-            out[AY], out[UV] = squared - uy * uy, ux * uy
-            for j, k in enumerate(FIRST_NEXT):
-                if j >= 3:
-                    first[NEXT + j, c, here, :] = out[k]
-
-    pipeline((static_shift, static_body), 0, chunks, G_STATIC)
-
-    def reader(source, keys, offset):
-        def at(k, c, rows_at):
-            return source[k, c, rows_at, :]
-
-        def right(k, c, rows_at):
-            return source[offset + keys.index(k), c, rows_at, :]
-
-        return at, right
-
-    f_at, f_right = reader(first, FIRST_NEXT, NEXT)
-    s_at, s_right = reader(second, SECOND_NEXT, SECOND_AT)
-
-    def face(step, dim, c, here, lm_l, lm_r, lp_l, lp_r):
-        low, high = jnp.minimum(lm_l, lm_r), jnp.maximum(lp_l, lp_r)
-        slow, fast = jnp.minimum(low, 0.0), jnp.maximum(high, 0.0)
-        inverse = 1.0 / (fast - slow)
-        masked = statics[FMX + dim, c, here, :] * inverse
-        alpha, beta = fast * masked, slow * masked
-        gamma = slow * alpha
-        e_slow = halved_on_tie(alpha * inverse, low < 0.0, low == 0.0)
-        e_fast = halved_on_tie(beta * inverse, high > 0.0, high == 0.0)
-        for k, value in enumerate((alpha, beta, gamma, slow, fast, e_slow, e_fast)):
-            faces[step, dim, k, c, here, :] = value
-        return alpha, beta, gamma
-
-    def coefs_of(step, dim, c, here):
-        return [faces[step, dim, k, c, here, :] for k in range(7)]
-
-    def crossing(coefs, flux_l, flux_r, held_l, held_r):
-        alpha, beta, gamma = coefs
-        return alpha * flux_l - beta * flux_r + gamma * (held_r - held_l)
-
-    def net_of(k, here):
-        values = [col_flux[k, c, here, :] for c in range(wide)]
-        return [mine - entering for mine, entering in zip(values, last_lanes(values))]
-
-    def first_cols(row):
-        here = pl.ds(row + TOP, 8)
-        for c in range(wide):
-            coefs = face(
-                0, 1, c, here, f_at(LMY, c, here), f_right(LMY, c, here),
-                f_at(LPY, c, here), f_right(LPY, c, here),
-            )
-            for k, (flux, held) in enumerate(((MY, H), (TT, MX), (QY, MY))):
-                col_flux[k, c, here, :] = crossing(
-                    coefs, f_at(flux, c, here), f_right(flux, c, here),
-                    f_at(held, c, here), f_right(held, c, here),
-                )
+    shift_whole, shift_outer = shift_stage(EVERY, EVERY), shift_stage(EVERY[tiles - 1 :], (0, tiles))
+    static_whole = static_stage(EVERY, EVERY, EVERY)
+    static_outer = static_stage(EVERY[tiles:], (0, *EVERY[tiles - 1 :]), EVERY[tiles - 1 :])
+    faces_whole, faces_outer = first_faces(EVERY, EVERY), first_faces(EVERY[tiles - 1 :], EVERY[tiles:])
+
+    def chosen(whole_stage, outer_stage, last_inner):
+        def stage(row, index):
+            inside = index is None or 1 <= index <= last_inner
+            (outer_stage if inside else whole_stage)(row)
+
+        return stage
+
+    pipeline(
+        (
+            chosen(shift_whole, shift_outer, chunks - 2),
+            chosen(static_whole, static_outer, chunks - 2),
+        ),
+        0, chunks, G_OUTER, begin=2, end=chunks - 1,
+    )
 
     def first_cells(row):
         start = row + TOP
-        here, after, before = pl.ds(start, 8), pl.ds(start + 1, 8), pl.ds(start - 1, 8)
+        here, before = pl.ds(start, 8), pl.ds(start - 1, 8)
         net = [net_of(k, here) for k in range(3)]
         for c in range(wide):
-            coefs = face(
-                0, 0, c, here, f_at(LMX, c, here), f_at(LMX, c, after),
-                f_at(LPX, c, here), f_at(LPX, c, after),
-            )
             new = []
-            for k, (flux, held) in enumerate(((MX, H), (QX, MX), (TT, MY))):
-                value = crossing(
-                    coefs, f_at(flux, c, here), f_at(flux, c, after),
-                    f_at(held, c, here), f_at(held, c, after),
-                )
-                row_flux[k, c, here, :] = value
+            for k in range(3):
+                value = row_flux[k, c, here, :]
                 change = value - row_flux[k, c, before, :] + net[k][c]
                 if k > 0:
                     change = change + f_at((None, WX, WY)[k], c, here)
@@ -619,16 +684,21 @@
         def shift(row):
             here = pl.ds(row + TOP, 8)
             for k in planes:
-                put_next(adj, TERM_R + k, here, {0: [adj[k, c, here, :] for c in range(wide)]})
+                values = [adj[k, c, here, :] for c in range(wide)]
+                for c, value in enumerate(next_lanes(values)):
+                    adj[TERM_R + k, c, here, :] = value
 
         return shift
 
-    pipeline((first_cols, first_cells, first_shift), 0, chunks, G_FIRST)
+    pipeline(
+        (chosen(faces_whole, faces_outer, chunks - 3), plain(first_cells), plain(first_shift)),
+        0, chunks, G_FIRST, begin=3, end=chunks - 2,
+    )
     if rounds > 1:
         learn(1)
         if rounds > 2:
             tell(2)
-    pipeline((last_cols, last_cells, adj_shift(TERM)), 0, chunks, G_LAST)
+    pipeline((plain(last_cols), plain(last_cells), plain(adj_shift(TERM))), 0, chunks, G_LAST)
 
     def depth_body(i, carry):
         start = pl.multiple_of(i * 8, 8)
@@ -694,7 +764,10 @@
             adj[ZX, c, here, :] = in_x[1]
             adj[ZY, c, here, :] = in_y[1]
 
-    pipeline((back_cols, back_cells, adj_shift(ADJ, ZX, ZY)), 0, chunks, G_BACK_LAST)
+    pipeline(
+        (plain(back_cols), plain(back_cells), plain(adj_shift(ADJ, ZX, ZY))),
+        0, chunks, G_BACK_LAST,
+    )
 
     own_hot = lax.broadcasted_iota(jnp.int32, (rows, dam_count), 0) == local_row
     stacked = []
@@ -787,13 +860,13 @@
                 pair(PY), pair(RY),
             )
 
-        turned = pltpu.roll(col_face(wide - 1)[1], 1, 1)
+        current = pltpu.roll(col_face(wide - 1)[1], 1, 1)
         for c in range(tiles):
             left, right = first_row_face(c, start)
             row_flux[0, c, here, :] = right
             left_y, right_y = col_face(c)
-            turned, last = pltpu.roll(right_y, 1, 1), turned
-            entering = jnp.where(lane == 0, last, turned)
+            current, last = pltpu.roll(right_y, 1, 1), current
+            entering = jnp.where(lane == 0, last, current)
             across = left + row_flux[0, c, before, :] + (left_y + entering)
             walls = adj[ZX, c, here, :] * f_at(BX, c, here) + adj[ZY, c, here, :] * f_at(BY, c, here)
             adjoint_out[pl.ds(row, 8), c * LANES : (c + 1) * LANES] = (

time: 23 us -> 22 us (0.957)
  Pallas kernels: 22.2 us -> 21.2 us
    pallas_call x1, Pallas kernels: 21.4 us -> 20.3 us  [on_device(): pl.pallas_call(functools.partial(kernel, n_gx, n_gy, cols * n_gy, damage_...]
where the time goes in v6:
time: 22 us; the launch traced here: 21.8 us
  Pallas kernels  21.2 us (96%)
  between operations  0.64 us (3%)
    pallas_call x1, Pallas kernels, on_device(): pl.pallas_call(functools.partial(kernel, n_gx, n_gy, cols * n_gy, damage_...  20.3 us
    pallas_call x1, Pallas kernels, on_device(): pl.pallas_call(place, out_shape=tuple((jax.ShapeDtypeStruct(value.shape,...  0.82 us

profile of v6, /device:TPU:0, one launch (start us, length us, event | category | flops | bytes accessed | tf_op | source)
XLA Modules:
  0.0 21.8 jit_solution(108258225321027836)
XLA Ops:
  0.6 20.3 %window.1 = (f32[128,512]{1,0:T(8,128)S(1)}, f32[128,512]{1,0:T(8,128)S(1)}, f32[2,64]{1,0:T(2,128)S(1)}) custom-call(f32[128,512]{1,0:T(8,128)} %depth_in.1, f32[128,512]{1,0:T(8,128)} %mx_in.1, f32[128,512]{1,0:T(8,128)} %my_in.1, s32[128,512]{1,0:T(8,128)} %wet_in.1, s32[128,512]{1,0:T(8,128)} %class_in.1, f32[8]{0:T(128)} %rates_in.1, s32[1,64]{1,0:T(1,128)} %bitcast.4, ...), custom_call_target="tpu_custom_call" | custom-call | tf_op jit(solution)/shard_map/window/pallas_call | solution.py:920
  21.0 0.8 %place.1 = (f32[128,512]{1,0:T(8,128)}, f32[128,512]{1,0:T(8,128)}, f32[2,64]{1,0:T(2,128)}) custom-call(f32[128,512]{1,0:T(8,128)S(1)} %get-tuple-element.9.refs_0_, f32[128,512]{1,0:T(8,128)S(1)} %get-tuple-element.10.refs_1_, f32[2,64]{1,0:T(2,128)S(1)} %get-tuple-element.11.refs_2_), custom_call_target="tpu_custom_call" | custom-call | tf_op jit(solution)/shard_map/place/pallas_call | solution.py:978

commit v7 on v6

--- a/solution.py
+++ b/solution.py
@@ -186,9 +186,9 @@
     for copy in small[1:]:
         copy.start()
 
-    for copy in loads:
+    small[0].wait()
+    for copy in loads[:10]:
         copy.wait()
-    small[0].wait()
 
     rate = [rates[k] for k in range(classes)]
 
@@ -206,12 +206,6 @@
             jnp.where(wet, weight, 0.0),
         )
 
-    for c in range(tiles):
-        for side, start, pick in ((0, 0, 0), (1, rows - 8, 4)):
-            four = coded_chunk(c, start)
-            for k in range(4):
-                send_rows[side, c, 4 * k : 4 * k + 4, :] = four[k][pick : pick + 4]
-
     def pack_body(i, carry):
         start = pl.multiple_of(i * 8, 8)
         left = coded_chunk(0, start)
@@ -225,7 +219,14 @@
         pack_cols[pl.ds(start, 8), :] = packed
         return carry
 
-    lax.fori_loop(0, rows // 8, pack_body, 0, unroll=2)
+    lax.fori_loop(0, rows // 8, pack_body, 0, unroll=4)
+    for copy in loads[10:]:
+        copy.wait()
+    for c in range(tiles):
+        for side, start, pick in ((0, 0, 0), (1, rows - 8, 4)):
+            four = coded_chunk(c, start)
+            for k in range(4):
+                send_rows[side, c, 4 * k : 4 * k + 4, :] = four[k][pick : pick + 4]
     turned = jnp.transpose(pack_cols[...])
     send_cols[0] = turned[0:16]
     send_cols[1] = turned[16:32]
@@ -270,7 +271,7 @@
             device_id_type=MESH,
         )
 
-    for index in (4, 5, 6, 7, 0, 1, 2, 3):
+    for index in (0, 1, 4, 5, 6, 7, 2, 3):
 
         @pl.when(sides[index][0])
         def _(index=index):
@@ -578,7 +579,7 @@
         put_start(tiles, start + OWN, 8, four)
         return carry
 
-    lax.fori_loop(0, rows // 8, rim_body, 0, unroll=2)
+    lax.fori_loop(0, rows // 8, rim_body, 0, unroll=4)
     for left_slot, right_slot, exists, at_rows, pick in (
         (0, 1, has_up, TOP, 4),
         (2, 3, has_down, OWN + rows, 0),
@@ -796,12 +797,14 @@
             tell(level + 1)
 
     count = n_gx * n_gy
+    me = ix * n_gy + iy
+    recv_all[me] = gpart[...]
 
     def send_grads(k, carry):
-        to = lax.rem(ix * n_gy + iy + 1 + k, count)
+        to = k + (k >= me).astype(jnp.int32)
         pltpu.make_async_remote_copy(
             src_ref=gpart,
-            dst_ref=recv_all.at[k],
+            dst_ref=recv_all.at[me],
             send_sem=grad_send.at[0],
             recv_sem=grad_recv.at[0],
             device_id=(lax.div(to, n_gy), lax.rem(to, n_gy)),
@@ -876,8 +879,9 @@
     sweep(backward_first, 0, rows // 8, G_BACK_FIRST)
 
     for sem in (grad_send, grad_recv):
-        pltpu.make_async_copy(recv_all, recv_all, sem.at[0]).wait()
-    total = gpart[...] + jnp.sum(recv_all[...], axis=0)
+        others = recv_all.at[pl.ds(0, count - 1)]
+        pltpu.make_async_copy(others, others, sem.at[0]).wait()
+    total = jnp.sum(recv_all[...], axis=0)
     for s in range(2):
         grad_out[s : s + 1, :] = total[:, s * dam_count : (s + 1) * dam_count]
 
@@ -949,7 +953,7 @@
             pltpu.VMEM((2, 16, rows), f32),
             pltpu.VMEM((4, 8, LANES), f32),
             pltpu.VMEM((1, 2 * dam_count), f32),
-            pltpu.VMEM((n_gx * n_gy - 1, 1, 2 * dam_count), f32),
+            pltpu.VMEM((n_gx * n_gy, 1, 2 * dam_count), f32),
             pltpu.SMEM(damage_rates.shape, f32),
             pltpu.VMEM((1, dam_count), jnp.int32),
             pltpu.VMEM(releases.shape[::-1], f32),

time: 22 us -> 21.3 us (0.968)
  Pallas kernels: 21.2 us -> 20.4 us
    pallas_call x1, Pallas kernels: 20.3 us -> 19.6 us  [on_device(): pl.pallas_call(functools.partial(kernel, n_gx, n_gy, cols * n_gy, damage_...]
where the time goes in v7:
time: 21.3 us; the launch traced here: 21.1 us
  Pallas kernels  20.4 us (96%)
  between operations  0.64 us (3%)
    pallas_call x1, Pallas kernels, on_device(): pl.pallas_call(functools.partial(kernel, n_gx, n_gy, cols * n_gy, damage_...  19.6 us
    pallas_call x1, Pallas kernels, on_device(): pl.pallas_call(place, out_shape=tuple((jax.ShapeDtypeStruct(value.shape,...  0.82 us

profile of v7, /device:TPU:0, one launch (start us, length us, event | category | flops | bytes accessed | tf_op | source)
XLA Modules:
  0.0 21.1 jit_solution(2243849604991833868)
XLA Ops:
  0.6 19.6 %window.1 = (f32[128,512]{1,0:T(8,128)S(1)}, f32[128,512]{1,0:T(8,128)S(1)}, f32[2,64]{1,0:T(2,128)S(1)}) custom-call(f32[128,512]{1,0:T(8,128)} %depth_in.1, f32[128,512]{1,0:T(8,128)} %mx_in.1, f32[128,512]{1,0:T(8,128)} %my_in.1, s32[128,512]{1,0:T(8,128)} %wet_in.1, s32[128,512]{1,0:T(8,128)} %class_in.1, f32[8]{0:T(128)} %rates_in.1, s32[1,64]{1,0:T(1,128)} %bitcast.4, ...), custom_call_target="tpu_custom_call" | custom-call | tf_op jit(solution)/shard_map/window/pallas_call | solution.py:924
  20.3 0.8 %place.1 = (f32[128,512]{1,0:T(8,128)}, f32[128,512]{1,0:T(8,128)}, f32[2,64]{1,0:T(2,128)}) custom-call(f32[128,512]{1,0:T(8,128)S(1)} %get-tuple-element.9.refs_0_, f32[128,512]{1,0:T(8,128)S(1)} %get-tuple-element.10.refs_1_, f32[2,64]{1,0:T(2,128)S(1)} %get-tuple-element.11.refs_2_), custom_call_target="tpu_custom_call" | custom-call | tf_op jit(solution)/shard_map/place/pallas_call | solution.py:982

commit v8 on v7

--- a/solution.py
+++ b/solution.py
@@ -14,7 +14,7 @@
 LANES = 128
 TOP = 8
 OWN = TOP + HALO
-G_STATIC, G_FACES, G_OUTER, G_FIRST, G_LAST, G_BACK_LAST, G_BACK_FIRST = 2, 2, 2, 3, 5, 3, 1
+G_STATIC, G_FACES, G_OUTER, G_FIRST, G_LAST, G_BACK_LAST, G_BACK_FIRST = 2, 2, 14, 6, 15, 5, 1
 MESH = pl.DeviceIdType.MESH
 
 
@@ -701,16 +701,6 @@
             tell(2)
     pipeline((plain(last_cols), plain(last_cells), plain(adj_shift(TERM))), 0, chunks, G_LAST)
 
-    def depth_body(i, carry):
-        start = pl.multiple_of(i * 8, 8)
-        for c in range(tiles):
-            own = pl.ds(start + OWN, 8)
-            depth_out[pl.ds(start, 8), c * LANES : (c + 1) * LANES] = jnp.where(
-                statics[WET, c, own, :] > 0.0, last_h[c, own, :], raw_d[c, pl.ds(start, 8), :]
-            )
-        return carry
-
-    lax.fori_loop(0, rows // 8, depth_body, 0)
     def last_face(coefs, lm, lp, h, n, z, p, r, ih):
         alpha, beta, gamma = coefs[:3]
         gh = z[1] - z[0]
@@ -771,25 +761,18 @@
     )
 
     own_hot = lax.broadcasted_iota(jnp.int32, (rows, dam_count), 0) == local_row
-    stacked = []
+    hots = jnp.concatenate([col_hot[...]] * 3, axis=0)
+    sums = []
     for plane in (ADJ, TERM):
         parts = [three_parts(adj[plane, c, OWN : OWN + rows, :]) for c in range(tiles)]
-        stacked.append(
-            jnp.concatenate([parts[c][k] for k in range(3) for c in range(tiles)], axis=1)
-        )
-    picked = lax.dot_general(
-        jnp.concatenate(stacked, axis=0), jnp.concatenate([col_hot[...]] * 3, axis=0),
-        (((1,), (0,)), ((), ())), preferred_element_type=jnp.float32,
-    )
-    gpart[...] = jnp.concatenate(
-        [
-            INFLOW_GAIN * jnp.sum(
-                jnp.where(own_hot, picked[s * rows : (s + 1) * rows], 0.0), axis=0, keepdims=True
-            )
-            for s in range(2)
-        ],
-        axis=1,
-    )
+        picked = lax.dot_general(
+            jnp.concatenate([parts[c][k] for k in range(3) for c in range(tiles)], axis=1), hots,
+            (((1,), (0,)), ((), ())), preferred_element_type=jnp.float32,
+        )
+        sums.append(
+            INFLOW_GAIN * jnp.sum(jnp.where(own_hot, picked, 0.0), axis=0, keepdims=True)
+        )
+    gpart[...] = jnp.concatenate(sums, axis=1)
 
     for level in range(2, rounds):
         learn(level)
@@ -813,6 +796,17 @@
         return carry
 
     lax.fori_loop(0, count - 1, send_grads, 0)
+
+    def depth_body(i, carry):
+        start = pl.multiple_of(i * 8, 8)
+        for c in range(tiles):
+            own = pl.ds(start + OWN, 8)
+            depth_out[pl.ds(start, 8), c * LANES : (c + 1) * LANES] = jnp.where(
+                statics[WET, c, own, :] > 0.0, last_h[c, own, :], raw_d[c, pl.ds(start, 8), :]
+            )
+        return carry
+
+    lax.fori_loop(0, rows // 8, depth_body, 0)
 
     def first_face(coefs, lm, lp, h, n, t, q, v, zh, zn, zt, a, uv, p, r):
         alpha, beta, gamma = coefs[:3]

time: 21.3 us -> 20.4 us (0.958)
  Pallas kernels: 20.4 us -> 19.6 us
    pallas_call x1, Pallas kernels: 19.6 us -> 18.8 us  [on_device(): pl.pallas_call(functools.partial(kernel, n_gx, n_gy, cols * n_gy, damage_...]
where the time goes in v8:
time: 20.4 us; the launch traced here: 20.2 us
  Pallas kernels  19.6 us (96%)
  between operations  0.64 us (3%)
    pallas_call x1, Pallas kernels, on_device(): pl.pallas_call(functools.partial(kernel, n_gx, n_gy, cols * n_gy, damage_...  18.8 us
    pallas_call x1, Pallas kernels, on_device(): pl.pallas_call(place, out_shape=tuple((jax.ShapeDtypeStruct(value.shape,...  0.82 us

profile of v8, /device:TPU:0, one launch (start us, length us, event | category | flops | bytes accessed | tf_op | source)
XLA Modules:
  0.0 20.2 jit_solution(11516085148424380810)
XLA Ops:
  0.6 18.8 %window.1 = (f32[128,512]{1,0:T(8,128)S(1)}, f32[128,512]{1,0:T(8,128)S(1)}, f32[2,64]{1,0:T(2,128)S(1)}) custom-call(f32[128,512]{1,0:T(8,128)} %depth_in.1, f32[128,512]{1,0:T(8,128)} %mx_in.1, f32[128,512]{1,0:T(8,128)} %my_in.1, s32[128,512]{1,0:T(8,128)} %wet_in.1, s32[128,512]{1,0:T(8,128)} %class_in.1, f32[8]{0:T(128)} %rates_in.1, s32[1,64]{1,0:T(1,128)} %bitcast.4, ...), custom_call_target="tpu_custom_call" | custom-call | tf_op jit(solution)/shard_map/window/pallas_call | solution.py:918
  19.4 0.8 %place.1 = (f32[128,512]{1,0:T(8,128)}, f32[128,512]{1,0:T(8,128)}, f32[2,64]{1,0:T(2,128)}) custom-call(f32[128,512]{1,0:T(8,128)S(1)} %get-tuple-element.9.refs_0_, f32[128,512]{1,0:T(8,128)S(1)} %get-tuple-element.10.refs_1_, f32[2,64]{1,0:T(2,128)S(1)} %get-tuple-element.11.refs_2_), custom_call_target="tpu_custom_call" | custom-call | tf_op jit(solution)/shard_map/place/pallas_call | solution.py:976

commit v9 on v8

--- a/solution.py
+++ b/solution.py
@@ -219,7 +219,7 @@
         pack_cols[pl.ds(start, 8), :] = packed
         return carry
 
-    lax.fori_loop(0, rows // 8, pack_body, 0, unroll=4)
+    lax.fori_loop(0, rows // 8, pack_body, 0, unroll=16)
     for copy in loads[10:]:
         copy.wait()
     for c in range(tiles):
@@ -579,7 +579,7 @@
         put_start(tiles, start + OWN, 8, four)
         return carry
 
-    lax.fori_loop(0, rows // 8, rim_body, 0, unroll=4)
+    lax.fori_loop(0, rows // 8, rim_body, 0, unroll=16)
     for left_slot, right_slot, exists, at_rows, pick in (
         (0, 1, has_up, TOP, 4),
         (2, 3, has_down, OWN + rows, 0),

time: 20.4 us -> 20 us (0.980)
  Pallas kernels: 19.6 us -> 19.2 us
    pallas_call x1, Pallas kernels: 18.8 us -> 18.4 us  [on_device(): pl.pallas_call(functools.partial(kernel, n_gx, n_gy, cols * n_gy, damage_...]
where the time goes in v9:
time: 20 us; the launch traced here: 19.8 us
  Pallas kernels  19.2 us (96%)
  between operations  0.64 us (3%)
    pallas_call x1, Pallas kernels, on_device(): pl.pallas_call(functools.partial(kernel, n_gx, n_gy, cols * n_gy, damage_...  18.4 us
    pallas_call x1, Pallas kernels, on_device(): pl.pallas_call(place, out_shape=tuple((jax.ShapeDtypeStruct(value.shape,...  0.82 us

profile of v9, /device:TPU:0, one launch (start us, length us, event | category | flops | bytes accessed | tf_op | source)
XLA Modules:
  0.0 19.8 jit_solution(18410093374821858051)
XLA Ops:
  0.6 18.4 %window.1 = (f32[128,512]{1,0:T(8,128)S(1)}, f32[128,512]{1,0:T(8,128)S(1)}, f32[2,64]{1,0:T(2,128)S(1)}) custom-call(f32[128,512]{1,0:T(8,128)} %depth_in.1, f32[128,512]{1,0:T(8,128)} %mx_in.1, f32[128,512]{1,0:T(8,128)} %my_in.1, s32[128,512]{1,0:T(8,128)} %wet_in.1, s32[128,512]{1,0:T(8,128)} %class_in.1, f32[8]{0:T(128)} %rates_in.1, s32[1,64]{1,0:T(1,128)} %bitcast.4, ...), custom_call_target="tpu_custom_call" | custom-call | tf_op jit(solution)/shard_map/window/pallas_call | solution.py:918
  19.0 0.8 %place.1 = (f32[128,512]{1,0:T(8,128)}, f32[128,512]{1,0:T(8,128)}, f32[2,64]{1,0:T(2,128)}) custom-call(f32[128,512]{1,0:T(8,128)S(1)} %get-tuple-element.9.refs_0_, f32[128,512]{1,0:T(8,128)S(1)} %get-tuple-element.10.refs_1_, f32[2,64]{1,0:T(2,128)S(1)} %get-tuple-element.11.refs_2_), custom_call_target="tpu_custom_call" | custom-call | tf_op jit(solution)/shard_map/place/pallas_call | solution.py:976

commit v10 on v9

--- a/solution.py
+++ b/solution.py
@@ -302,7 +302,7 @@
             put_start(c, start + OWN, 8, coded_chunk(c, start))
         return carry
 
-    lax.fori_loop(0, rows // 8, own_body, 0)
+    lax.fori_loop(0, rows // 8, own_body, 0, unroll=4)
 
     for copy in small[1:]:
         copy.wait()
@@ -910,7 +910,7 @@
     high = rows + 2 * HALO + 2 * TOP
     dam_count = dam_cell.shape[0]
     f32 = jnp.float32
-    plane = (wide, high, LANES)
+    plane = (wide + 1, high, LANES)
     own = (tiles, rows, LANES)
     anywhere = pl.BlockSpec(memory_space=pl.ANY)
     vmem = pl.BlockSpec(memory_space=pltpu.VMEM)

time: 20 us -> 20 us (level)
  no operation moved by 1% of the time
where the time goes in v10:
time: 20 us; the launch traced here: 19.8 us
  Pallas kernels  19.1 us (96%)
  between operations  0.64 us (3%)
    pallas_call x1, Pallas kernels, on_device(): pl.pallas_call(functools.partial(kernel, n_gx, n_gy, cols * n_gy, damage_...  18.3 us
    pallas_call x1, Pallas kernels, on_device(): pl.pallas_call(place, out_shape=tuple((jax.ShapeDtypeStruct(value.shape,...  0.82 us

profile of v10, /device:TPU:0, one launch (start us, length us, event | category | flops | bytes accessed | tf_op | source)
XLA Modules:
  0.0 19.8 jit_solution(9606608632592830658)
XLA Ops:
  0.6 18.3 %window.1 = (f32[128,512]{1,0:T(8,128)S(1)}, f32[128,512]{1,0:T(8,128)S(1)}, f32[2,64]{1,0:T(2,128)S(1)}) custom-call(f32[128,512]{1,0:T(8,128)} %depth_in.1, f32[128,512]{1,0:T(8,128)} %mx_in.1, f32[128,512]{1,0:T(8,128)} %my_in.1, s32[128,512]{1,0:T(8,128)} %wet_in.1, s32[128,512]{1,0:T(8,128)} %class_in.1, f32[8]{0:T(128)} %rates_in.1, s32[1,64]{1,0:T(1,128)} %bitcast.4, ...), custom_call_target="tpu_custom_call" | custom-call | tf_op jit(solution)/shard_map/window/pallas_call | solution.py:918
  18.9 0.8 %place.1 = (f32[128,512]{1,0:T(8,128)}, f32[128,512]{1,0:T(8,128)}, f32[2,64]{1,0:T(2,128)}) custom-call(f32[128,512]{1,0:T(8,128)S(1)} %get-tuple-element.9.refs_0_, f32[128,512]{1,0:T(8,128)S(1)} %get-tuple-element.10.refs_1_, f32[2,64]{1,0:T(2,128)S(1)} %get-tuple-element.11.refs_2_), custom_call_target="tpu_custom_call" | custom-call | tf_op jit(solution)/shard_map/place/pallas_call | solution.py:976
